TPU v7x, 128 devices: a whole 4x4x4 slice. The times are simulated.
128 devices in a mesh: ctx: 16 (over y, z_hi, core), tp: 8 (over z_lo, x).
Axes of the slice: x: 4, y: 4, z: 4 (z_hi: 2, z_lo: 2; z = z_hi * 2 + z_lo), core: 2. Of those that a mesh axis runs over, the one named last changes fastest.
Arguments:
- prompt_states: bfloat16 [2048, 1024], P('ctx'), may hold values from -1.5 to 1.5
- segment_ids: int32 [2048], P('ctx'), may hold values from 0 to 3, never falling along the last dimension, each value on 1 to 1024 neighbouring positions
- past_keys: bfloat16 [2048, 1024], P('ctx', 'tp'), may hold values from -1024 to 1024
- past_values: bfloat16 [2048, 1024], P('ctx', 'tp'), may hold values from -6 to 6
- cache_request: int32 [2048], P('ctx'), may hold values from 0 to 2, as said below
- decode_ids: int32 [4], replicated, may hold values from 0 to 32127
- embed_table: bfloat16 [32128, 1024], P(('ctx', 'tp')), may hold values from -6 to 6
- attn_gain: bfloat16 [1024], replicated, may hold values from 0.25 to 1.75
- ff_gain: bfloat16 [1024], replicated, may hold values from 0.25 to 1.75
- final_gain: bfloat16 [1024], replicated, may hold values from 0.25 to 1.75
- w_query: bfloat16 [1024, 1024], P(None, 'tp'), may hold values from -0.1875 to 0.1875
- w_key: bfloat16 [1024, 1024], P(None, 'tp'), may hold values from -0.1875 to 0.1875
- w_value: bfloat16 [1024, 1024], P(None, 'tp'), may hold values from -0.1875 to 0.1875
- w_out: bfloat16 [1024, 1024], P('tp'), may hold values from -0.1875 to 0.1875
- w_gate: bfloat16 [1024, 2816], P(None, 'tp'), may hold values from -0.1875 to 0.1875
- w_up: bfloat16 [1024, 2816], P(None, 'tp'), may hold values from -0.1875 to 0.1875
- w_down: bfloat16 [2816, 1024], P('tp'), may hold values from -0.109375 to 0.109375
- lm_head: bfloat16 [1024, 32128], P(None, ('ctx', 'tp')), may hold values from -0.1875 to 0.1875
Outputs:
- prompt_out: bfloat16 [2048, 1024], P('ctx')
- logits: float32 [4, 32128], P(None, ('ctx', 'tp'))
- relaid_keys: bfloat16 [2048, 1024], P(('ctx', 'tp'))
- relaid_values: bfloat16 [2048, 1024], P(('ctx', 'tp'))
Inputs may be any that keep to these rules, and one draw needn't show every extreme that they name: `cache_request`: only the even requests have cached rows, which may lie on any devices. `segment_ids`: the tokens of a request are consecutive; a request holds at most 1024 of them, and one request holds exactly that many.
All inputs are finite; a program needn't handle non-finite values.
Results may differ from a plain program's by a relative error of at most 0.03.
Values may be sent and summed in bfloat16 or wider, within the bound.
A program may use at most 64 MiB of HBM per device.

v0:
```python
import jax
import jax.numpy as jnp
from jax import lax
from jax.sharding import PartitionSpec as P

DH = 64


epsilon = 1e-06
scale_factor = 0.125
negative = -1e30


def joined(part, axis, combine):
    gathered = jax.tree.map(lambda a: lax.all_gather(a, axis), part)

    def take(source):
        return jax.tree.map(lambda a: lax.dynamic_index_in_dim(a, source, 0, False), gathered)

    return lax.fori_loop(
        1, lax.axis_size(axis), lambda source, state: combine(state, take(source)), take(0)
    )


def rms_norm(states, gain):
    states = states.astype(jnp.float32)
    mean_square = jnp.mean(states * states, axis=-1, keepdims=True)
    return (states * lax.rsqrt(mean_square + epsilon) * gain.astype(jnp.float32)).astype(
        jnp.bfloat16
    )


def partial_attend(queries, keys, values, allowed):
    scores = (
        jnp.einsum("qhd,khd->qhk", queries, keys, preferred_element_type=jnp.float32) * scale_factor
    )
    scores = jnp.where(allowed[:, None, :], scores, negative)
    highest = jnp.max(scores, axis=2)
    weights = jnp.where(allowed[:, None, :], jnp.exp(scores - highest[:, :, None]), 0.0)
    weight_sum = jnp.sum(weights, axis=2)
    summed = jnp.einsum(
        "qhk,khd->qhd", weights.astype(jnp.bfloat16), values, preferred_element_type=jnp.float32
    )
    return (highest, weight_sum, summed)


def join_parts(earlier, latter):
    highest = jnp.maximum(earlier[0], latter[0])
    left_scale = jnp.exp(earlier[0] - highest)
    right_scale = jnp.exp(latter[0] - highest)
    weight_sum = earlier[1] * left_scale + latter[1] * right_scale
    summed = earlier[2] * left_scale[:, :, None] + latter[2] * right_scale[:, :, None]
    return (highest, weight_sum, summed)


def finish(partials):
    return (partials[2] / partials[1][:, :, None]).astype(jnp.bfloat16)


def fold_block(running, query_heads, block_keys, block_values, allowed):
    key_count = block_keys.shape[0]
    head_group = query_heads.shape[1]

    def attend(current):
        return join_parts(
            current,
            partial_attend(
                query_heads,
                block_keys.reshape(key_count, head_group, DH),
                block_values.reshape(key_count, head_group, DH),
                allowed,
            ),
        )

    def unchanged(current):
        return current

    return lax.cond(jnp.any(allowed), attend, unchanged, running)


def gated_units(normed, w_gate, w_up, w_down):
    gate_value = jnp.dot(normed, w_gate, preferred_element_type=jnp.float32)
    up_value = jnp.dot(normed, w_up, preferred_element_type=jnp.float32)
    hidden = (jax.nn.gelu(gate_value, approximate=True) * up_value).astype(jnp.bfloat16)
    return jnp.dot(hidden, w_down, preferred_element_type=jnp.float32)


def project(normed, weight):
    return jnp.dot(normed, weight, preferred_element_type=jnp.float32).astype(jnp.bfloat16)


def on_device(
    prompt_states,
    segment_ids,
    past_keys,
    past_values,
    cache_request,
    decode_ids,
    embed_table,
    attn_gain,
    ff_gain,
    final_gain,
    w_query,
    w_key,
    w_value,
    w_out,
    w_gate,
    w_up,
    w_down,
    lm_head,
):
    row_count = prompt_states.shape[0]
    head_group = w_query.shape[1] // DH
    ctx_index = lax.axis_index("ctx")
    normed = rms_norm(prompt_states, attn_gain)
    queries = project(normed, w_query)
    keys = project(normed, w_key)
    values = project(normed, w_value)
    query_heads = queries.reshape(row_count, head_group, DH)
    q_positions = ctx_index * row_count + jnp.arange(row_count, dtype=jnp.int32)
    start_parts = (
        jnp.full((row_count, head_group), negative, jnp.float32),
        jnp.zeros((row_count, head_group), jnp.float32),
        jnp.zeros((row_count, head_group, DH), jnp.float32),
    )
    block_keys = lax.all_gather(keys, "ctx", axis=0, tiled=True)
    block_values = lax.all_gather(values, "ctx", axis=0, tiled=True)
    block_segment = lax.all_gather(segment_ids, "ctx", axis=0, tiled=True)
    key_positions = jnp.arange(block_segment.shape[0], dtype=jnp.int32)
    partials = fold_block(
        start_parts,
        query_heads,
        block_keys,
        block_values,
        (segment_ids[:, None] == block_segment[None, :])
        & (key_positions[None, :] <= q_positions[:, None]),
    )
    block_keys = lax.all_gather(past_keys, "ctx", axis=0, tiled=True)
    block_values = lax.all_gather(past_values, "ctx", axis=0, tiled=True)
    block_segment = lax.all_gather(cache_request, "ctx", axis=0, tiled=True)
    partials = fold_block(
        partials,
        query_heads,
        block_keys,
        block_values,
        segment_ids[:, None] == block_segment[None, :],
    )
    attended = finish(partials).reshape(row_count, head_group * DH)
    head_term = jnp.dot(attended, w_out, preferred_element_type=jnp.float32)
    residual = prompt_states.astype(jnp.float32) + lax.psum(
        head_term.astype(jnp.bfloat16), "tp"
    ).astype(jnp.float32)
    unit_term = gated_units(rms_norm(residual, ff_gain), w_gate, w_up, w_down)
    prompt_out = (
        residual + lax.psum(unit_term.astype(jnp.bfloat16), "tp").astype(jnp.float32)
    ).astype(jnp.bfloat16)
    relaid_keys, relaid_values = (
        lax.all_to_all(keys, "tp", split_axis=0, concat_axis=1, tiled=True),
        lax.all_to_all(values, "tp", split_axis=0, concat_axis=1, tiled=True),
    )
    vocab_rows = embed_table.shape[0]
    vocab_start = lax.axis_index(("ctx", "tp")) * vocab_rows
    one_hot = (
        decode_ids[:, None] == vocab_start + jnp.arange(vocab_rows, dtype=jnp.int32)[None, :]
    ).astype(jnp.bfloat16)
    embedded = lax.psum(
        jnp.dot(one_hot, embed_table, preferred_element_type=jnp.float32), ("ctx", "tp")
    )
    request_count = decode_ids.shape[0]
    decode_normed = rms_norm(embedded, attn_gain)
    decode_queries = project(decode_normed, w_query)
    decode_heads = decode_queries.reshape(request_count, head_group, DH)
    decode_keys = project(decode_normed, w_key).reshape(request_count, head_group, DH)
    decode_values = project(decode_normed, w_value).reshape(request_count, head_group, DH)
    requests = jnp.arange(request_count, dtype=jnp.int32)
    cache_count = past_keys.shape[0]
    cache_part = partial_attend(
        decode_heads,
        past_keys.reshape(cache_count, head_group, DH),
        past_values.reshape(cache_count, head_group, DH),
        requests[:, None] == cache_request[None, :],
    )
    prompt_part = partial_attend(
        decode_heads,
        keys.reshape(row_count, head_group, DH),
        values.reshape(row_count, head_group, DH),
        requests[:, None] == segment_ids[None, :],
    )
    gathered = joined(join_parts(prompt_part, cache_part), "ctx", join_parts)
    own_part = partial_attend(
        decode_heads, decode_keys, decode_values, requests[:, None] == requests[None, :]
    )
    decode_attended = finish(join_parts(gathered, own_part)).reshape(request_count, head_group * DH)
    decode_residual = embedded + lax.psum(
        jnp.dot(decode_attended, w_out, preferred_element_type=jnp.float32), "tp"
    )
    decode_term = gated_units(rms_norm(decode_residual, ff_gain), w_gate, w_up, w_down)
    decode_final = decode_residual + lax.psum(decode_term, "tp")
    logits = jnp.dot(
        rms_norm(decode_final, final_gain), lm_head, preferred_element_type=jnp.float32
    )
    return (prompt_out, logits, relaid_keys, relaid_values)


def solution(mesh):
    placed = (
        P("ctx", None),
        P("ctx"),
        P("ctx", "tp"),
        P("ctx", "tp"),
        P("ctx"),
        P(),
        P(("ctx", "tp"), None),
        P(),
        P(),
        P(),
        P(None, "tp"),
        P(None, "tp"),
        P(None, "tp"),
        P("tp", None),
        P(None, "tp"),
        P(None, "tp"),
        P("tp", None),
        P(None, ("ctx", "tp")),
    )
    return jax.shard_map(
        on_device,
        mesh=mesh,
        in_specs=placed,
        out_specs=(
            P("ctx", None),
            P(None, ("ctx", "tp")),
            P(("ctx", "tp"), None),
            P(("ctx", "tp"), None),
        ),
        check_vma=False,
    )
```

profile of v0, /device:TPU:0, one launch (start us, length us, event | category | flops | bytes accessed | tf_op | source)
XLA Modules:
  0.0 462.5 jit_solution(8723615287294162902)
XLA Ops:
  7.3 25.5 %all-gather.2 = s32[16,1,128]{2,1,0:T(1,128)S(1)} all-gather(s32[1,1,128]{2,1,0:T(1,128)} %bitcast.173), channel_id=1, replica_groups=mesh['ctx'=16,'tp'=8] {'ctx'}, dimensions={0}, use_global_device_ids=true | all-gather | bytes 8704 | tf_op jit(solution)/shard_map/all_gather | solution.py:128
  32.8 19.3 %all-gather.1 = s32[16,1,128]{2,1,0:T(1,128)S(1)} all-gather(s32[1,1,128]{2,1,0:T(1,128)} %bitcast.174), channel_id=1, replica_groups=mesh['ctx'=16,'tp'=8] {'ctx'}, dimensions={0}, use_global_device_ids=true | all-gather | bytes 8704 | tf_op jit(solution)/shard_map/all_gather | solution.py:140
  52.1 3.4 fusion.125
  56.8 0.7 convert_element_type.100
  57.4 1.1 fusion.44
  58.5 1.9 convolution_convert_fusion.4
  60.5 23.8 %all_gather.34 = bf16[2048,128]{1,0:T(8,128)(2,1)S(1)} all-gather(bf16[128,128]{1,0:T(8,128)(2,1)} %convolution_convert_fusion.4), channel_id=1, replica_groups=mesh['ctx'=16,'tp'=8] {'ctx'}, dimensions={0}, use_global_device_ids=true | all-gather | bytes 557056 | tf_op jit(solution)/shard_map/all_gather | solution.py:126
  84.6 0.9 convolution_convert_fusion.2
  85.5 22.3 %all_gather.35 = bf16[2048,128]{1,0:T(8,128)(2,1)} all-gather(bf16[128,128]{1,0:T(8,128)(2,1)} %convolution_convert_fusion.2), channel_id=1, replica_groups=mesh['ctx'=16,'tp'=8] {'ctx'}, dimensions={0}, use_global_device_ids=true | all-gather | bytes 557056 | tf_op jit(solution)/shard_map/all_gather | solution.py:127
  108.0 25.2 %all_gather.36 = bf16[2048,128]{0,1:T(8,128)(2,1)} all-gather(bf16[128,128]{0,1:T(8,128)(2,1)S(1)} %copy.75), channel_id=1, replica_groups=mesh['ctx'=16,'tp'=8] {'ctx'}, dimensions={0}, use_global_device_ids=true | all-gather | bytes 557056 | tf_op jit(solution)/shard_map/all_gather | solution.py:138
  133.3 22.1 %all_gather.37 = bf16[2048,128]{0,1:T(8,128)(2,1)} all-gather(bf16[128,128]{0,1:T(8,128)(2,1)S(1)} %copy.76), channel_id=1, replica_groups=mesh['ctx'=16,'tp'=8] {'ctx'}, dimensions={0}, use_global_device_ids=true | all-gather | bytes 557056 | tf_op jit(solution)/shard_map/all_gather | solution.py:139
  155.4 8.3 %conditional.2 = (f32[128,2]{0,1:T(2,128)}, f32[128,2]{0,1:T(2,128)S(1)}, f32[128,2,64]{0,2,1:T(8,128)S(1)}) conditional(s32[]{:T(128)} %convert_element_type.99, () %tuple.45, (pred[128,2048]{0,1:T(8,128)(4,1)}, bf16[2048,128]{1,0:T(8,128)(2,1)S(1)}, bf16[128,2,64]{0,2,1:T(8,128)(2,1)S(1)}, bf16[2048,128]{1,0:T(8,128)(2,1)}) %tuple.100), branch_computations={%region_3.4_spmd, %region_4.7_spmd} | conditional | flops 138970624 | bytes 11384884 | solution.py:78
  155.4 1.0 copy.73
  156.5 1.8 fusion.131
  158.2 0.6 exponential_multiply_fusion
  159.2 0.7 multiply_add_fusion
  159.9 2.1 copy.74
  162.0 1.7 fusion.5
  163.8 3.6 conditional.3
  163.8 1.8 fusion.132
  165.6 0.4 fusion.14
  166.0 0.7 multiply_add_fusion.1
  166.7 0.7 fusion.16
  167.4 1.0 convolution_convert_fusion.1
  168.4 4.9 %all-to-all-start = ((bf16[8,16,128]{2,1,0:T(8,128)(2,1)}), bf16[8,16,128]{2,1,0:T(8,128)(2,1)S(1)}, u32[]{:S(2)}, u32[]{:S(2)}) async-start(bf16[8,16,128]{2,1,0:T(8,128)(2,1)} %bitcast.34), calls=%async_computation | async-start | bytes 65536 | tf_op jit(solution)/shard_map/all_to_all | solution.py:158
  173.4 0.9 copy.77
  174.3 0.9 copy.81
  175.4 66.9 %psum.37 = f32[4,1024]{1,0:T(4,128)S(1)} all-reduce(f32[4,1024]{1,0:T(4,128)S(1)} %fusion.70), channel_id=1, replica_groups=mesh['ctx'=16,'tp'=8] {'ctx','tp'}, use_global_device_ids=true, to_apply=%region_14.15 | all-reduce | flops 4096 | bytes 32768 | tf_op jit(solution)/shard_map/psum | solution.py:166
  242.5 1.1 convolution_convert_fusion.7
  243.6 1.1 convolution_convert_fusion.6
  244.8 1.2 convolution_convert_fusion.5
  246.8 22.7 %all_gather.38 = f32[16,4,2]{1,2,0:T(2,128)S(1)} all-gather(f32[1,4,2]{1,2,0:T(2,128)S(1)} %get-tuple-element.301), channel_id=1, replica_groups=mesh['ctx'=16,'tp'=8] {'ctx'}, dimensions={0}, use_global_device_ids=true | all-gather | bytes 544 | tf_op jit(solution)/shard_map/all_gather | solution.py:15
  269.5 19.2 %all_gather.39 = f32[16,4,2]{1,2,0:T(2,128)S(1)} all-gather(f32[1,4,2]{1,2,0:T(2,128)S(1)} %get-tuple-element.300), channel_id=1, replica_groups=mesh['ctx'=16,'tp'=8] {'ctx'}, dimensions={0}, use_global_device_ids=true | all-gather | bytes 544 | tf_op jit(solution)/shard_map/all_gather | solution.py:15
  289.1 22.3 %all-gather = f32[64,2,64]{2,1,0:T(2,128)S(1)} all-gather(f32[4,2,64]{2,1,0:T(2,128)S(1)} %copy.83), channel_id=2, replica_groups=mesh['ctx'=16,'tp'=8] {'ctx'}, dimensions={0}, use_global_device_ids=true | all-gather | bytes 34816 | tf_op jit(solution)/shard_map/all_gather | solution.py:15
  311.4 4.4 while.19
  316.6 31.3 %psum.38 = f32[4,1024]{1,0:T(4,128)S(1)} all-reduce(f32[4,1024]{1,0:T(4,128)S(1)} %fusion.136), channel_id=1, replica_groups=mesh['ctx'=16,'tp'=8] {'tp'}, use_global_device_ids=true, to_apply=%region_24.25 | all-reduce | flops 4096 | bytes 32768 | tf_op jit(solution)/shard_map/psum | solution.py:194
  348.4 0.7 fusion.42
  349.0 30.6 %psum.39 = f32[4,1024]{1,0:T(4,128)S(1)} all-reduce(f32[4,1024]{1,0:T(4,128)S(1)} %fusion.42), channel_id=1, replica_groups=mesh['ctx'=16,'tp'=8] {'tp'}, use_global_device_ids=true, to_apply=%region_26.27 | all-reduce | flops 4096 | bytes 32768 | tf_op jit(solution)/shard_map/psum | solution.py:198
  379.8 0.8 fusion.59
  380.6 1.2 multiply_reduce_fusion
  381.8 1.4 fusion.120
  383.2 1.7 convolution_convert_fusion
  384.9 3.3 all-to-all-start.1
  388.3 0.6 copy_bitcast_fusion.1
  388.9 5.6 %all-to-all-done.1 = bf16[8,16,128]{2,1,0:T(8,128)(2,1)S(1)} async-done(((bf16[8,16,128]{2,1,0:T(8,128)(2,1)}), bf16[8,16,128]{2,1,0:T(8,128)(2,1)S(1)}, u32[]{:S(2)}, u32[]{:S(2)}) %all-to-all-start.1) | async-done | bytes 32800 | tf_op jit(solution)/shard_map/all_to_all | solution.py:159
  394.5 0.6 copy_bitcast_fusion
  395.1 58.8 %all-reduce.5.cloned.1.call-done = bf16[128,1024]{1,0:T(8,128)(2,1)} async-done(((bf16[128,1024]{1,0:T(8,128)(2,1)}), bf16[128,1024]{1,0:T(8,128)(2,1)}) %all-reduce.5.cloned.1.call-update) | async-done | bytes 262160 | tf_op jit(solution)/shard_map/psum | solution.py:155
  453.9 1.8 add_convert_fusion
  (149 shorter events, 8.6 us)
Async XLA Ops:
  7.2 341.2 %copy-start = (bf16[352,1024]{1,0:T(8,128)(2,1)S(1)}, bf16[352,1024]{1,0:T(8,128)(2,1)}, u32[]{:S(2)}) copy-start(bf16[352,1024]{1,0:T(8,128)(2,1)} %param.40) | copy-start | bytes 2162692
  7.2 77.1 %copy-start.1 = (bf16[128,1024]{1,0:T(8,128)(2,1)S(1)}, bf16[128,1024]{1,0:T(8,128)(2,1)}, u32[]{:S(2)}) copy-start(bf16[128,1024]{1,0:T(8,128)(2,1)} %param.24) | copy-start | bytes 786436
  7.2 77.1 %copy-start.10 = (bf16[1024,128]{1,0:T(8,128)(2,1)S(1)}, bf16[1024,128]{1,0:T(8,128)(2,1)}, u32[]{:S(2)}) copy-start(bf16[1024,128]{1,0:T(8,128)(2,1)} %param.34) | copy-start | bytes 786436
  7.2 77.4 %copy-start.11 = (bf16[1024,128]{1,0:T(8,128)(2,1)S(1)}, bf16[1024,128]{1,0:T(8,128)(2,1)}, u32[]{:S(2)}) copy-start(bf16[1024,128]{1,0:T(8,128)(2,1)} %param.36) | copy-start | bytes 786436
  7.2 100.6 %copy-start.12 = (bf16[128,128]{1,0:T(8,128)(2,1)S(1)}, bf16[128,128]{1,0:T(8,128)(2,1)}, u32[]{:S(2)}) copy-start(bf16[128,128]{1,0:T(8,128)(2,1)} %param.26) | copy-start | bytes 98308
  7.2 373.4 %all-reduce.3.cloned.1.call-start = ((), (), s32[]{:S(2)}) async-start(), calls=%async_computation.2 | async-start | bytes 524288 | tf_op jit(solution)/shard_map/psum | solution.py:150
  55.5 77.7 %copy-start.13 = (bf16[128,128]{1,0:T(8,128)(2,1)S(1)}, bf16[128,128]{1,0:T(8,128)(2,1)}, u32[]{:S(2)}) copy-start(bf16[128,128]{1,0:T(8,128)(2,1)} %param.27) | copy-start | bytes 98308
  156.4 2.4 copy-start.5
  163.7 3.7 copy-start.6
  163.7 9.7 %copy-start.18 = (s32[128]{0:T(128)S(1)}, s32[128]{0:T(128)}, u32[]{:S(2)}) copy-start(s32[128]{0:T(128)} %param.28) | copy-start | bytes 1540
  163.7 10.5 %copy-start.16 = (s32[128]{0:T(128)S(1)}, s32[128]{0:T(128)}, u32[]{:S(2)}) copy-start(s32[128]{0:T(128)} %param.25) | copy-start | bytes 1540
  163.7 11.4 %copy-start.7 = (bf16[251,1024]{1,0:T(8,128)(2,1)S(1)}, bf16[251,1024]{1,0:T(8,128)(2,1)}, u32[]{:S(2)}) copy-start(bf16[251,1024]{1,0:T(8,128)(2,1)} %param.30) | copy-start | bytes 1542148
  163.7 11.4 %copy-start.17 = (s32[4]{0:T(128)S(1)}, s32[4]{0:T(128)}, u32[]{:S(2)}) copy-start(s32[4]{0:T(128)} %param.29) | copy-start | bytes 52
  163.8 2.9 copy-start.9
  167.4 78.5 %copy-start.14 = (bf16[1024]{0:T(1024)(128)(2,1)S(1)}, bf16[1024]{0:T(1024)(128)(2,1)}, u32[]{:S(2)}) copy-start(bf16[1024]{0:T(1024)(128)(2,1)} %param.32) | copy-start | bytes 6148
  167.4 180.7 %copy-start.3 = (bf16[1024,352]{0,1:T(8,128)(2,1)S(1)}, bf16[1024,352]{0,1:T(8,128)(2,1)}, u32[]{:S(2)}) copy-start(bf16[1024,352]{0,1:T(8,128)(2,1)} %param.38) | copy-start | bytes 2162692
  168.4 180.0 %copy-start.4 = (bf16[1024,352]{0,1:T(8,128)(2,1)S(1)}, bf16[1024,352]{0,1:T(8,128)(2,1)}, u32[]{:S(2)}) copy-start(bf16[1024,352]{0,1:T(8,128)(2,1)} %param.39) | copy-start | bytes 2162692
  168.4 216.5 %all-to-all-start = ((bf16[8,16,128]{2,1,0:T(8,128)(2,1)}), bf16[8,16,128]{2,1,0:T(8,128)(2,1)S(1)}, u32[]{:S(2)}, u32[]{:S(2)}) async-start(bf16[8,16,128]{2,1,0:T(8,128)(2,1)} %bitcast.34), calls=%async_computation | async-start | bytes 65536 | tf_op jit(solution)/shard_map/all_to_all | solution.py:158
  173.3 280.5 %all-reduce.5.cloned.1.call-start = ((), (), s32[]{:S(2)}) async-start(), calls=%async_computation.3 | async-start | bytes 524288 | tf_op jit(solution)/shard_map/psum | solution.py:155
  244.7 135.1 %copy-start.15 = (bf16[1024]{0:T(1024)(128)(2,1)S(1)}, bf16[1024]{0:T(1024)(128)(2,1)}, u32[]{:S(2)}) copy-start(bf16[1024]{0:T(1024)(128)(2,1)} %param.33) | copy-start | bytes 6148
  244.7 135.1 %copy-start.8 = (bf16[1024,251]{1,0:T(8,128)(2,1)S(1)}, bf16[1024,251]{1,0:T(8,128)(2,1)}, u32[]{:S(2)}) copy-start(bf16[1024,251]{1,0:T(8,128)(2,1)} %param.41) | copy-start | bytes 1542148
  380.6 2.6 copy-start.2
  384.9 9.5 %all-to-all-start.1 = ((bf16[8,16,128]{2,1,0:T(8,128)(2,1)}), bf16[8,16,128]{2,1,0:T(8,128)(2,1)S(1)}, u32[]{:S(2)}, u32[]{:S(2)}) async-start(bf16[8,16,128]{2,1,0:T(8,128)(2,1)} %bitcast.36), calls=%async_computation.1 | async-start | bytes 65536 | tf_op jit(solution)/shard_map/all_to_all | solution.py:159
Sparse Core Ops, SparseCore 0:
  168.5 73.1 all-reduce.2
  385.0 68.7 all-reduce.4
where the time goes:
time: 464 us; the launch traced here: 462 us
  blocking collectives  331 us (71%)
  waiting for transfers between devices  64.4 us (14%)
  matrix products  19.7 us (4%)
  between operations  15.7 us (3%)
  other arithmetic  13.4 us (3%)
  local copies, waits for them, and re-layouts  9.55 us (2%)
  starting transfers between devices  8.32 us (2%)
    psum x1, blocking collectives, on_device(): lax.psum(jnp.dot(one_hot, embed_table, preferred_element_type=jnp.float32...  66.9 us
    all_gather x3, blocking collectives, joined(): gathered = jax.tree.map(lambda a: lax.all_gather(a, axis), part)  64.2 us
    psum x1, waiting for transfers between devices, on_device(): lax.psum(unit_term.astype(jnp.bfloat16), 'tp').astype(jnp.float32)  58.8 us
    psum x1, blocking collectives, on_device(): lax.psum(jnp.dot(decode_attended, w_out, preferred_element_type=jnp.float...  31.3 us
    psum x1, blocking collectives, on_device(): decode_final = decode_residual + lax.psum(decode_term, 'tp')  30.6 us
    all_gather x1, blocking collectives, on_device(): block_segment = lax.all_gather(segment_ids, 'ctx', axis=0, tiled=True)  25.5 us
    all_gather x1, blocking collectives, on_device(): block_keys = lax.all_gather(past_keys, 'ctx', axis=0, tiled=True)  25.2 us
    all_gather x1, blocking collectives, on_device(): block_keys = lax.all_gather(keys, 'ctx', axis=0, tiled=True)  23.8 us
  transfers between devices with their start and end apart: 4, of which 2 were waited for; matrix products, arithmetic and copies ran while one was open for 4% of the time, Pallas kernels for 0%

commit v1 on v0

v1 whole, which is shorter than its diff:
```python
import jax
import jax.numpy as jnp
from jax import lax
from jax.experimental import pallas as pl
from jax.experimental.pallas import tpu as pltpu
from jax.sharding import PartitionSpec as P

DH = 64
EPS = 1e-06
NEG = -1e30
FLOOR = -1e29
MESH = pl.DeviceIdType.MESH
F32 = jnp.float32
BF16 = jnp.bfloat16


def dot(a, b):
    return jnp.dot(a, b, preferred_element_type=F32)


def dot_nt(a, b):
    return lax.dot_general(a, b, (((1,), (1,)), ((), ())), preferred_element_type=F32)


def norm(states, gain):
    mean_square = jnp.mean(states * states, axis=-1, keepdims=True)
    return (states * lax.rsqrt(mean_square + EPS) * gain).astype(BF16)


def kernel(
    ids_ref, x_hbm, seg_hbm, pk_hbm, pv_hbm, creq_hbm, emb_hbm,
    ag_hbm, fg_hbm, lg_hbm, wq_hbm, wk_hbm, wv_hbm, wo_hbm, wg_hbm, wu_hbm, wd_hbm, lm_hbm,
    out_ref, logits_ref, relk_ref, relv_ref,
    x_v, ag_v, fg_v, lg_v, wq_v, wk_v, wv_v, wo_v, wg_v, wu_v, wd_v, lm_v, emb_v, pv_v,
    idown, vrow, kid_s, s_s, p_s, osend, stsend, dsend, part_s, nbuf, decp_s, e1src, e2src, fin_s,
    kbuf, vtbuf, qbuf, idy, idz, obuf, stbuf, dbuf, e1buf, e2buf, rs1buf, ar1buf, rs2buf, ar2buf,
    lsem, ksend, krecv, qsend, qrecv, isend, irecv, e1send, e1recv, e2send, e2recv,
    rlsend, rlrecv, osems, orecv, dsems, drecv, tsend, trecv,
):
    c = lax.axis_index("ctx")
    t = lax.axis_index("tp")
    y = lax.div(c, 4)
    zc = lax.rem(c, 4)

    def ypeer(d):
        return (lax.rem(y + d, 4) * 4 + zc, t)

    def zpeer(e):
        return (y * 4 + lax.rem(zc + e, 4), t)

    def tpeer(r):
        return (c, lax.rem(t + r, 8))

    def cpeer(k):
        return (lax.rem(c + k, 16), t)

    def remote(src, dst, ssem, rsem, peer):
        return pltpu.make_async_remote_copy(
            src_ref=src, dst_ref=dst, send_sem=ssem, recv_sem=rsem,
            device_id=peer, device_id_type=MESH,
        )

    barrier = pltpu.get_barrier_semaphore()
    for k in range(1, 16):
        pl.semaphore_signal(barrier, 1, device_id=cpeer(k), device_id_type=MESH)
    for r in range(1, 8):
        pl.semaphore_signal(barrier, 1, device_id=tpeer(r), device_id_type=MESH)

    loads = {}
    todo = [
        ("x", x_hbm, x_v), ("ag", ag_hbm, ag_v), ("wk", wk_hbm, wk_v), ("wv", wv_hbm, wv_v),
        ("wq", wq_hbm, wq_v), ("pk", pk_hbm, kbuf.at[pl.ds(128, 128)]), ("pv", pv_hbm, pv_v),
        ("seg", seg_hbm, idown.at[0]), ("creq", creq_hbm, idown.at[1]),
        ("emb", emb_hbm, emb_v), ("wo", wo_hbm, wo_v), ("fg", fg_hbm, fg_v),
        ("wg", wg_hbm, wg_v), ("wu", wu_hbm, wu_v), ("wd", wd_hbm, wd_v),
        ("lg", lg_hbm, lg_v), ("lm", lm_hbm, lm_v),
    ]
    for i, (name, src, dst) in enumerate(todo):
        loads[name] = pltpu.make_async_copy(src, dst, lsem.at[i])
        loads[name].start()

    def gain_of(ref):
        return ref[...].astype(F32).reshape(1, 1024)

    loads["x"].wait()
    loads["ag"].wait()
    a_gain = gain_of(ag_v)
    normed = norm(x_v[...].astype(F32), a_gain)
    loads["wk"].wait()
    kbuf[0:128, :] = dot(normed, wk_v[...]).astype(BF16)
    loads["wv"].wait()
    values = dot(normed, wv_v[...])
    vrow[...] = values.astype(BF16)
    vtbuf[:, 0:128] = values.T.astype(BF16)
    loads["wq"].wait()
    queries = dot(normed, wq_v[...]).astype(BF16).astype(F32) * 0.125
    qbuf[0] = queries.T.astype(BF16)
    loads["pk"].wait()
    loads["pv"].wait()
    vtbuf[:, 128:256] = pv_v[...].astype(F32).T.astype(BF16)
    loads["seg"].wait()
    loads["creq"].wait()

    first_row = (c * 8 + t) * 251
    row16 = lax.broadcasted_iota(jnp.int32, (16, 251), 0)
    col16 = lax.broadcasted_iota(jnp.int32, (16, 251), 1) + first_row
    wanted = jnp.full((16, 251), -1, jnp.int32)
    for q in range(4):
        wanted = jnp.where(row16 == q, ids_ref[q], wanted)
    one_hot = (col16 == wanted).astype(F32).astype(BF16)
    loads["emb"].wait()
    e1src[...] = dot(one_hot, emb_v[...])[0:4].astype(BF16)

    pl.semaphore_wait(barrier, 22)

    kv_copies = []
    for d in range(1, 4):
        kv_copies.append(remote(
            kbuf.at[pl.ds(0, 256)], kbuf.at[pl.ds(256 * d, 256)],
            ksend.at[d, 0], krecv.at[d, 0], ypeer(d)))
        kv_copies.append(remote(
            vtbuf.at[:, pl.ds(0, 256)], vtbuf.at[:, pl.ds(256 * d, 256)],
            ksend.at[d, 1], krecv.at[d, 1], ypeer(d)))
        kv_copies.append(remote(idown, idy.at[d], isend.at[0, d], irecv.at[0, d], ypeer(d)))
    q_copies = []
    for e in range(1, 4):
        q_copies.append(remote(qbuf.at[0], qbuf.at[e], qsend.at[e], qrecv.at[e], zpeer(e)))
        q_copies.append(remote(idown, idz.at[e], isend.at[1, e], irecv.at[1, e], zpeer(e)))
    for copy in kv_copies + q_copies:
        copy.start()
    e1_copies = []
    for k in range(1, 16):
        e1_copies.append(remote(e1src, e1buf.at[k], e1send.at[k], e1recv.at[k], cpeer(k)))
    for copy in e1_copies:
        copy.start()

    my_columns = pl.ds(pl.multiple_of(t * 128, 128), 128)
    my_rows = pl.ds(pl.multiple_of(t * 16, 16), 16)
    rel_copies = []
    for r in range(1, 8):
        other = pl.ds(pl.multiple_of(lax.rem(t + r, 8) * 16, 16), 16)
        rel_copies.append(remote(
            kbuf.at[other], relk_ref.at[:, my_columns], rlsend.at[0, r], rlrecv.at[0, r], tpeer(r)))
        rel_copies.append(remote(
            vrow.at[other], relv_ref.at[:, my_columns], rlsend.at[1, r], rlrecv.at[1, r], tpeer(r)))
    for copy in rel_copies:
        copy.start()
    relk_ref[:, my_columns] = kbuf[my_rows, :]
    relv_ref[:, my_columns] = vrow[my_rows, :]

    total = e1src[...].astype(F32)
    for k in range(1, 16):
        e1_copies[k - 1].wait()
        total = total + e1buf[k].astype(F32)
    e2src[...] = total.astype(BF16)
    e2_copies = []
    for r in range(1, 8):
        e2_copies.append(remote(e2src, e2buf.at[r], e2send.at[r], e2recv.at[r], tpeer(r)))
        e2_copies[-1].start()

    for copy in kv_copies:
        copy.wait()
    idy[0] = idown[...]
    idz[0] = idown[...]
    id_rows = []
    for d in range(4):
        id_rows.append(idy[d, 0:1, :].astype(F32))
        id_rows.append(idy[d, 1:2, :].astype(F32))
    id_columns = jnp.concatenate(id_rows + [jnp.zeros((120, 128), F32)], axis=0).T
    for b in range(8):
        kid_s[b] = jnp.broadcast_to(id_columns[:, b : b + 1], (128, 128))
    for copy in q_copies:
        copy.wait()

    k_iota = lax.broadcasted_iota(jnp.int32, (128, 128), 0)
    q_iota = lax.broadcasted_iota(jnp.int32, (128, 128), 1)

    def attend(i, _):
        e = lax.rem(i + 1, 4)
        qt = qbuf[e]
        top = qt[0:64, :]
        low = qt[64:128, :]
        zero = jnp.zeros((64, 128), BF16)
        qd = jnp.concatenate(
            [jnp.concatenate([top, zero], axis=1), jnp.concatenate([zero, low], axis=1)], axis=0)
        qid = idz[e, 0:1, :].astype(F32)
        q_at = y * 512 + lax.rem(zc - e + 4, 4) * 128
        highest = jnp.full((8, 256), FLOOR, F32)
        for b in range(8):
            s = dot(kbuf[b * 128 : (b + 1) * 128, :], qd)
            ok = kid_s[b] == qid
            if b % 2 == 0:
                k_at = lax.rem(y - b // 2 + 4, 4) * 512 + zc * 128
                ok = ok & (k_iota + (k_at - q_at) <= q_iota)
            s = jnp.where(jnp.concatenate([ok, ok], axis=1), s, NEG)
            s_s[b * 128 : (b + 1) * 128, :] = s
            highest = jnp.maximum(highest, jnp.max(s.reshape(16, 8, 256), axis=0))
        m = jnp.max(highest, axis=0, keepdims=True)
        total_w = jnp.zeros((8, 256), F32)
        for b in range(8):
            w = jnp.exp(s_s[b * 128 : (b + 1) * 128, :] - m)
            total_w = total_w + jnp.sum(w.reshape(16, 8, 256), axis=0)
            p_s[b * 128 : (b + 1) * 128, :] = w.astype(BF16)
        l = jnp.sum(total_w, axis=0, keepdims=True)
        o = dot(vtbuf[...], p_s[...])
        f = lax.rem(4 - e, 4)
        osend[f] = jnp.concatenate([o[0:64, 0:128], o[64:128, 128:256]], axis=0).astype(BF16)
        stsend[f] = jnp.concatenate(
            [m[:, 0:128], m[:, 128:256], l[:, 0:128], l[:, 128:256], jnp.zeros((4, 128), F32)],
            axis=0)

        @pl.when(i < 3)
        def _():
            remote(osend.at[f], obuf.at[f], osems.at[0, f], orecv.at[0, f], zpeer(f)).start()
            remote(stsend.at[f], stbuf.at[f], osems.at[1, f], orecv.at[1, f], zpeer(f)).start()

        return 0

    lax.fori_loop(0, 4, attend, 0)
    obuf[0] = osend[0]
    stbuf[0] = stsend[0]

    total = e2src[...].astype(F32)
    for r in range(1, 8):
        e2_copies[r - 1].wait()
        total = total + e2buf[r].astype(F32)
    embedded = total
    d_normed = jnp.concatenate(
        [norm(embedded, a_gain).astype(F32), jnp.zeros((12, 1024), F32)], axis=0).astype(BF16)
    dq = dot(d_normed, wq_v[...]).astype(BF16).astype(F32)[0:4] * 0.125
    dk = dot(d_normed, wk_v[...]).astype(BF16).astype(F32)[0:4]
    dv = dot(d_normed, wv_v[...]).astype(BF16).astype(F32)[0:4]
    lane4 = lax.broadcasted_iota(jnp.int32, (4, 128), 1)
    qd8 = jnp.concatenate(
        [jnp.where(lane4 < 64, dq, 0.0), jnp.where(lane4 >= 64, dq, 0.0)], axis=0)
    qd16 = jnp.concatenate([qd8, jnp.zeros((8, 128), F32)], axis=0).astype(BF16)
    k_ids = jnp.concatenate(id_rows, axis=1)
    rid = (lax.broadcasted_iota(jnp.int32, (16, 1024), 0) % 4).astype(F32)
    s = jnp.where(rid == k_ids, dot_nt(qd16, kbuf[...]), NEG)
    m = jnp.maximum(jnp.max(s, axis=1, keepdims=True), FLOOR)
    w = jnp.exp(s - m)
    l = jnp.sum(w, axis=1, keepdims=True)
    o = dot_nt(w.astype(BF16), vtbuf[...])
    dsend[0:8, :] = o[0:8]
    dsend[8:16, :] = jnp.broadcast_to(m[0:8], (8, 128))
    dsend[16:24, :] = jnp.broadcast_to(l[0:8], (8, 128))
    d_copies = []
    for e in range(1, 4):
        d_copies.append(remote(dsend, dbuf.at[e], dsems.at[e], drecv.at[e], zpeer(e)))
        d_copies[-1].start()

    for f in range(1, 4):
        remote(osend.at[f], obuf.at[f], osems.at[0, f], orecv.at[0, f], zpeer(f)).wait()
        remote(stsend.at[f], stbuf.at[f], osems.at[1, f], orecv.at[1, f], zpeer(f)).wait()
    stats = [stbuf[f] for f in range(4)]
    tops = [st[0:2] for st in stats]
    joint = jnp.maximum(jnp.maximum(tops[0], tops[1]), jnp.maximum(tops[2], tops[3]))
    scales = [jnp.exp(tp_ - joint) for tp_ in tops]
    weight = sum(sc * st[2:4] for sc, st in zip(scales, stats))
    inverse = 1.0 / weight
    attended = jnp.zeros((128, 128), F32)
    for f in range(4):
        factor = scales[f] * inverse
        spread = jnp.concatenate(
            [jnp.broadcast_to(factor[0:1], (64, 128)), jnp.broadcast_to(factor[1:2], (64, 128))],
            axis=0)
        attended = attended + obuf[f].astype(F32) * spread
    loads["wo"].wait()
    head_term = dot(attended.T.astype(BF16), wo_v[...])
    part_s[...] = head_term.astype(BF16)
    rs1_copies = []
    for r in range(1, 8):
        other = pl.ds(pl.multiple_of(lax.rem(t + r, 8) * 16, 16), 16)
        rs1_copies.append(remote(
            part_s.at[other], rs1buf.at[r], tsend.at[0, r], trecv.at[0, r], tpeer(r)))
        rs1_copies[-1].start()

    own_m = jnp.sum(qd8 * jnp.concatenate([dk, dk], axis=0), axis=1, keepdims=True)
    own_m = jnp.broadcast_to(own_m, (8, 128))
    for copy in d_copies:
        copy.wait()
    dparts = [dsend[...]] + [dbuf[e] for e in range(1, 4)]
    joint = own_m
    for part in dparts:
        joint = jnp.maximum(joint, part[8:16])
    own_scale = jnp.exp(own_m - joint)
    weight = own_scale
    summed = own_scale * jnp.concatenate([dv, dv], axis=0)
    for part in dparts:
        scale = jnp.exp(part[8:16] - joint)
        weight = weight + scale * part[16:24]
        summed = summed + scale * part[0:8]
    summed = summed / weight
    d_attended = jnp.where(lane4 < 64, summed[0:4], summed[4:8])
    d_attended = jnp.concatenate([d_attended, jnp.zeros((12, 128), F32)], axis=0).astype(BF16)
    d_term = dot(d_attended, wo_v[...])[0:4]
    decp_s[0] = d_term.astype(BF16)
    ar1_copies = []
    for r in range(1, 8):
        ar1_copies.append(remote(
            decp_s.at[0], ar1buf.at[r], tsend.at[1, r], trecv.at[1, r], tpeer(r)))
        ar1_copies[-1].start()

    residual = x_v[my_rows, :].astype(F32) + part_s[my_rows, :].astype(F32)
    for r in range(1, 8):
        rs1_copies[r - 1].wait()
        residual = residual + rs1buf[r].astype(F32)
    loads["fg"].wait()
    f_gain = gain_of(fg_v)
    nbuf[my_rows, :] = norm(residual, f_gain)
    ag1_copies = []
    for r in range(1, 8):
        ag1_copies.append(remote(
            nbuf.at[my_rows], nbuf.at[my_rows], tsend.at[2, r], trecv.at[2, r], tpeer(r)))
        ag1_copies[-1].start()
    fin_s[...] = residual

    d_residual = embedded + decp_s[0].astype(F32)
    for r in range(1, 8):
        ar1_copies[r - 1].wait()
        d_residual = d_residual + ar1buf[r].astype(F32)
    nbuf[128:144, :] = jnp.concatenate(
        [norm(d_residual, f_gain).astype(F32), jnp.zeros((12, 1024), F32)], axis=0).astype(BF16)

    loads["wg"].wait()
    loads["wu"].wait()
    loads["wd"].wait()
    for copy in ag1_copies:
        copy.wait()
    gate = dot(nbuf[...], wg_v[...])
    up = dot(nbuf[...], wu_v[...])
    hidden = (jax.nn.gelu(gate, approximate=True) * up).astype(BF16)
    unit_term = dot(hidden, wd_v[...])
    part_s[...] = unit_term[0:128].astype(BF16)
    decp_s[1] = unit_term[128:132].astype(BF16)
    rs2_copies = []
    for r in range(1, 8):
        other = pl.ds(pl.multiple_of(lax.rem(t + r, 8) * 16, 16), 16)
        rs2_copies.append(remote(
            part_s.at[other], rs2buf.at[r], tsend.at[3, r], trecv.at[3, r], tpeer(r)))
        rs2_copies[-1].start()
    ar2_copies = []
    for r in range(1, 8):
        ar2_copies.append(remote(
            decp_s.at[1], ar2buf.at[r], tsend.at[4, r], trecv.at[4, r], tpeer(r)))
        ar2_copies[-1].start()

    final = fin_s[...] + part_s[my_rows, :].astype(F32)
    for r in range(1, 8):
        rs2_copies[r - 1].wait()
        final = final + rs2buf[r].astype(F32)
    out_ref[my_rows, :] = final.astype(BF16)
    ag2_copies = []
    for r in range(1, 8):
        ag2_copies.append(remote(
            out_ref.at[my_rows], out_ref.at[my_rows], tsend.at[5, r], trecv.at[5, r], tpeer(r)))
        ag2_copies[-1].start()

    d_final = d_residual + decp_s[1].astype(F32)
    for r in range(1, 8):
        ar2_copies[r - 1].wait()
        d_final = d_final + ar2buf[r].astype(F32)
    loads["lg"].wait()
    loads["lm"].wait()
    l_normed = jnp.concatenate(
        [norm(d_final, gain_of(lg_v)).astype(F32), jnp.zeros((12, 1024), F32)], axis=0).astype(BF16)
    logits_ref[...] = dot(l_normed, lm_v[...])[0:4]

    for copy in rel_copies + ag2_copies:
        copy.wait()


def on_device(
    prompt_states, segment_ids, past_keys, past_values, cache_request, decode_ids, embed_table,
    attn_gain, ff_gain, final_gain, w_query, w_key, w_value, w_out, w_gate, w_up, w_down, lm_head,
):
    anywhere = pl.BlockSpec(memory_space=pl.ANY)
    vmem = pl.BlockSpec(memory_space=pltpu.VMEM)
    dma = pltpu.SemaphoreType.DMA
    local = [
        ((128, 1024), BF16), ((1024,), BF16), ((1024,), BF16), ((1024,), BF16),
        ((1024, 128), BF16), ((1024, 128), BF16), ((1024, 128), BF16), ((128, 1024), BF16),
        ((1024, 352), BF16), ((1024, 352), BF16), ((352, 1024), BF16), ((1024, 251), BF16),
        ((251, 1024), BF16), ((128, 128), BF16),
        ((8, 128), jnp.int32), ((128, 128), BF16), ((8, 128, 128), F32), ((1024, 256), F32),
        ((1024, 256), BF16), ((4, 128, 128), BF16), ((4, 8, 128), F32), ((24, 128), F32),
        ((128, 1024), BF16), ((144, 1024), BF16), ((2, 4, 1024), BF16), ((4, 1024), BF16),
        ((4, 1024), BF16), ((16, 1024), F32),
    ]
    arriving = [
        ((1024, 128), BF16), ((128, 1024), BF16), ((4, 128, 128), BF16), ((4, 8, 128), jnp.int32),
        ((4, 8, 128), jnp.int32), ((4, 128, 128), BF16), ((4, 8, 128), F32), ((4, 24, 128), F32),
        ((16, 4, 1024), BF16), ((8, 4, 1024), BF16), ((8, 16, 1024), BF16), ((8, 4, 1024), BF16),
        ((8, 16, 1024), BF16), ((8, 4, 1024), BF16),
    ]
    semaphores = [
        dma((17,)), dma((4, 2)), dma((4, 2)), dma((4,)), dma((4,)), dma((2, 4)), dma((2, 4)),
        dma((16,)), dma((16,)), dma((8,)), dma((8,)), dma((2, 8)), dma((2, 8)),
        dma((2, 4)), dma((2, 4)), dma((4,)), dma((4,)), dma((6, 8)), dma((6, 8)),
    ]
    return pl.pallas_call(
        kernel,
        out_shape=(
            jax.ShapeDtypeStruct((128, 1024), BF16),
            jax.ShapeDtypeStruct((4, 251), F32),
            jax.ShapeDtypeStruct((16, 1024), BF16),
            jax.ShapeDtypeStruct((16, 1024), BF16),
        ),
        in_specs=[pl.BlockSpec(memory_space=pltpu.SMEM)] + [anywhere] * 17,
        out_specs=(vmem, vmem, vmem, vmem),
        scratch_shapes=[pltpu.VMEM(s, d) for s, d in local + arriving] + semaphores,
        compiler_params=pltpu.CompilerParams(
            collective_id=0, has_side_effects=True, vmem_limit_bytes=48 * 1024 * 1024),
    )(
        decode_ids, prompt_states, segment_ids, past_keys, past_values, cache_request, embed_table,
        attn_gain, ff_gain, final_gain, w_query, w_key, w_value, w_out, w_gate, w_up, w_down,
        lm_head,
    )


def solution(mesh):
    placed = (
        P("ctx", None),
        P("ctx"),
        P("ctx", "tp"),
        P("ctx", "tp"),
        P("ctx"),
        P(),
        P(("ctx", "tp"), None),
        P(),
        P(),
        P(),
        P(None, "tp"),
        P(None, "tp"),
        P(None, "tp"),
        P("tp", None),
        P(None, "tp"),
        P(None, "tp"),
        P("tp", None),
        P(None, ("ctx", "tp")),
    )
    return jax.shard_map(
        on_device,
        mesh=mesh,
        in_specs=placed,
        out_specs=(
            P("ctx", None),
            P(None, ("ctx", "tp")),
            P(("ctx", "tp"), None),
            P(("ctx", "tp"), None),
        ),
        check_vma=False,
    )
```

time: 464 us -> 60 us (0.13)
  blocking collectives: 331 us -> 0 us
  waiting for transfers between devices: 64.4 us -> 0 us
  Pallas kernels: 0 us -> 48.2 us
  matrix products: 19.7 us -> 0 us
  between operations: 15.7 us -> 0.84 us
  other arithmetic: 13.4 us -> 0 us
  starting transfers between devices: 8.32 us -> 0 us
    all_gather x9 -> x0, blocking collectives: 202 us -> none  [the longest x3 64.2 us: joined(): gathered = jax.tree.map(lambda a: lax.all_gather(a, axis), part)]
    psum x3 -> x0, blocking collectives: 129 us -> none  [the longest x1 66.9 us: on_device(): lax.psum(jnp.dot(one_hot, embed_table, preferred_element_type=jnp.float32...]
    psum x2 -> x0, waiting for transfers between devices: 58.8 us -> none  [the longest x1 58.8 us: on_device(): lax.psum(unit_term.astype(jnp.bfloat16), 'tp').astype(jnp.float32)]
    pallas_call x0 -> x1, Pallas kernels: none -> 48.2 us  [on_device(): pl.pallas_call(kernel, out_shape=(jax.ShapeDtypeStruct((128, 1024), BF16)...]
    dot_general x24 -> x0, matrix products: 19.7 us -> none  [the longest x6 6.52 us: project(): jnp.dot(normed, weight, preferred_element_type=jnp.float32)]
    unnamed x36 -> x38, local copies, waits for them, and re-layouts: 0.31 us -> 10.4 us
    all_to_all x2 -> x0, starting transfers between devices: 8.24 us -> none  [the longest x1 4.89 us: on_device(): lax.all_to_all(keys, 'tp', split_axis=0, concat_axis=1, tiled=True)]
    all_to_all x2 -> x0, waiting for transfers between devices: 5.57 us -> none  [the longest x1 5.57 us: on_device(): lax.all_to_all(values, 'tp', split_axis=0, concat_axis=1, tiled=True)]
  transfers between devices with their start and end apart: 4 -> 0, of which waited for: 2 -> 0; matrix products, arithmetic and copies ran while one was open for 4% -> 0% of each run, Pallas kernels for 0% -> 0%
where the time goes in v1:
time: 60 us; the launch traced here: 59.5 us
  Pallas kernels  48.2 us (80%)
  local copies, waits for them, and re-layouts  10.4 us (17%)
  between operations  0.84 us (1%)
    pallas_call x1, Pallas kernels, on_device(): pl.pallas_call(kernel, out_shape=(jax.ShapeDtypeStruct((128, 1024), BF16)...  48.2 us
    unnamed x38, local copies, waits for them, and re-layouts  10.4 us

profile of v1, /device:TPU:0, one launch (start us, length us, event | category | flops | bytes accessed | tf_op | source)
XLA Modules:
  0.0 59.5 jit_solution(8155217446137968835)
XLA Ops:
  0.6 0.0 copy-start.2
  0.6 1.5 %copy.22.wg_hbm = bf16[1024,352]{1,0:T(8,128)(2,1)S(1)} copy(bf16[1024,352]{0,1:T(8,128)(2,1)} %param.32) | data formatting | bytes 1441792 | tf_op args[14]
  2.2 0.0 copy-start
  2.2 0.0 copy-start.1
  2.2 0.0 copy-start.8
  2.2 0.0 copy-start.9
  2.2 0.0 copy-start.10
  2.2 0.0 copy-start.11
  2.2 0.0 copy-start.12
  2.3 0.0 copy-start.13
  2.3 0.0 copy-start.14
  2.3 0.0 copy-start.15
  2.3 1.5 %copy.23.wu_hbm = bf16[1024,352]{1,0:T(8,128)(2,1)S(1)} copy(bf16[1024,352]{0,1:T(8,128)(2,1)} %param.33) | data formatting | bytes 1441792 | tf_op args[15]
  3.8 0.0 copy-done.2
  3.8 0.0 copy-done
  3.9 0.0 copy-done.1
  3.9 0.0 copy-done.8
  3.9 0.0 copy-done.9
  3.9 0.0 copy-done.10
  3.9 0.0 copy-done.11
  3.9 0.0 copy-done.12
  3.9 0.0 copy-done.13
  3.9 0.0 copy-done.14
  3.9 0.0 copy-done.15
  3.9 0.0 copy-start.3
  4.0 0.9 %copy-done.3 = bf16[128,1024]{1,0:T(8,128)(2,1)S(1)} copy-done((bf16[128,1024]{1,0:T(8,128)(2,1)S(1)}, bf16[128,1024]{1,0:T(8,128)(2,1)}, u32[]{:S(2)}) %copy-start.3) | copy-done | bytes 262168
  4.9 0.0 copy-start.4
  4.9 0.9 %copy-done.4 = bf16[1024,128]{1,0:T(8,128)(2,1)S(1)} copy-done((bf16[1024,128]{1,0:T(8,128)(2,1)S(1)}, bf16[1024,128]{1,0:T(8,128)(2,1)}, u32[]{:S(2)}) %copy-start.4) | copy-done | bytes 262168
  5.8 0.0 copy-start.5
  5.9 0.9 %copy-done.5 = bf16[1024,128]{1,0:T(8,128)(2,1)S(1)} copy-done((bf16[1024,128]{1,0:T(8,128)(2,1)S(1)}, bf16[1024,128]{1,0:T(8,128)(2,1)}, u32[]{:S(2)}) %copy-start.5) | copy-done | bytes 262168
  6.8 0.0 copy-start.6
  6.8 0.9 %copy-done.6 = bf16[1024,128]{1,0:T(8,128)(2,1)S(1)} copy-done((bf16[1024,128]{1,0:T(8,128)(2,1)S(1)}, bf16[1024,128]{1,0:T(8,128)(2,1)}, u32[]{:S(2)}) %copy-start.6) | copy-done | bytes 262168
  7.8 0.0 copy-start.7
  7.8 0.9 %copy-done.7 = bf16[128,1024]{1,0:T(8,128)(2,1)S(1)} copy-done((bf16[128,1024]{1,0:T(8,128)(2,1)S(1)}, bf16[128,1024]{1,0:T(8,128)(2,1)}, u32[]{:S(2)}) %copy-start.7) | copy-done | bytes 262168
  8.7 48.2 %shard_map.201 = (bf16[128,1024]{1,0:T(8,128)(2,1)S(1)}, f32[4,251]{1,0:T(4,128)S(1)}, bf16[16,1024]{1,0:T(8,128)(2,1)S(1)}, bf16[16,1024]{1,0:T(8,128)(2,1)S(1)}) custom-call(s32[4]{0:T(128)S(1)} %copy-done.13, bf16[128,1024]{1,0:T(8,128)(2,1)S(1)} %copy-done.3, s32[128]{0:T(128)S(1)} %copy-done.14, bf16[128,128]{1,0:T(8,128)(2,1)S(1)} %copy-done.8, ...), custom_call_target="tpu_custom_call" | custom-call | tf_op jit(solution)/shard_map/pallas_call | solution.py:401
  56.9 0.7 %copy.28 = bf16[128,1024]{1,0:T(8,128)(2,1)} copy(bf16[128,1024]{1,0:T(8,128)(2,1)S(1)} %get-tuple-element.8) | data formatting | bytes 524288
  57.6 0.6 copy.29
  58.2 0.6 %copy.30 = bf16[16,1024]{1,0:T(8,128)(2,1)} copy(bf16[16,1024]{1,0:T(8,128)(2,1)S(1)} %get-tuple-element.10) | data formatting | bytes 65536
  58.8 0.6 %copy.31 = bf16[16,1024]{1,0:T(8,128)(2,1)} copy(bf16[16,1024]{1,0:T(8,128)(2,1)S(1)} %get-tuple-element.11) | data formatting | bytes 65536
Async XLA Ops:
  0.6 3.2 %copy-start.2 = (bf16[1024,251]{1,0:T(8,128)(2,1)S(1)}, bf16[1024,251]{1,0:T(8,128)(2,1)}, u32[]{:S(2)}) copy-start(bf16[1024,251]{1,0:T(8,128)(2,1)} %lm_hbm.1) | copy-start | bytes 1542148
  2.2 1.7 %copy-start = (bf16[352,1024]{1,0:T(8,128)(2,1)S(1)}, bf16[352,1024]{1,0:T(8,128)(2,1)}, u32[]{:S(2)}) copy-start(bf16[352,1024]{1,0:T(8,128)(2,1)} %wd_hbm.1) | copy-start | bytes 2162692
  2.2 1.7 %copy-start.1 = (bf16[251,1024]{1,0:T(8,128)(2,1)S(1)}, bf16[251,1024]{1,0:T(8,128)(2,1)}, u32[]{:S(2)}) copy-start(bf16[251,1024]{1,0:T(8,128)(2,1)} %emb_hbm.1) | copy-start | bytes 1542148
  2.2 1.7 %copy-start.8 = (bf16[128,128]{1,0:T(8,128)(2,1)S(1)}, bf16[128,128]{1,0:T(8,128)(2,1)}, u32[]{:S(2)}) copy-start(bf16[128,128]{1,0:T(8,128)(2,1)} %pk_hbm.1) | copy-start | bytes 98308
  2.2 1.7 %copy-start.9 = (bf16[128,128]{1,0:T(8,128)(2,1)S(1)}, bf16[128,128]{1,0:T(8,128)(2,1)}, u32[]{:S(2)}) copy-start(bf16[128,128]{1,0:T(8,128)(2,1)} %pv_hbm.1) | copy-start | bytes 98308
  2.2 1.7 %copy-start.10 = (bf16[1024]{0:T(1024)(128)(2,1)S(1)}, bf16[1024]{0:T(1024)(128)(2,1)}, u32[]{:S(2)}) copy-start(bf16[1024]{0:T(1024)(128)(2,1)} %ag_hbm.1) | copy-start | bytes 6148
  2.2 1.7 %copy-start.11 = (bf16[1024]{0:T(1024)(128)(2,1)S(1)}, bf16[1024]{0:T(1024)(128)(2,1)}, u32[]{:S(2)}) copy-start(bf16[1024]{0:T(1024)(128)(2,1)} %fg_hbm.1) | copy-start | bytes 6148
  2.2 1.7 %copy-start.12 = (bf16[1024]{0:T(1024)(128)(2,1)S(1)}, bf16[1024]{0:T(1024)(128)(2,1)}, u32[]{:S(2)}) copy-start(bf16[1024]{0:T(1024)(128)(2,1)} %lg_hbm.1) | copy-start | bytes 6148
  2.3 1.7 %copy-start.13 = (s32[4]{0:T(128)S(1)}, s32[4]{0:T(128)}, u32[]{:S(2)}) copy-start(s32[4]{0:T(128)} %ids_ref.1) | copy-start | bytes 52
  2.3 1.7 %copy-start.14 = (s32[128]{0:T(128)S(1)}, s32[128]{0:T(128)}, u32[]{:S(2)}) copy-start(s32[128]{0:T(128)} %seg_hbm.1) | copy-start | bytes 1540
  2.3 1.7 %copy-start.15 = (s32[128]{0:T(128)S(1)}, s32[128]{0:T(128)}, u32[]{:S(2)}) copy-start(s32[128]{0:T(128)} %creq_hbm.1) | copy-start | bytes 1540
  3.9 1.0 %copy-start.3 = (bf16[128,1024]{1,0:T(8,128)(2,1)S(1)}, bf16[128,1024]{1,0:T(8,128)(2,1)}, u32[]{:S(2)}) copy-start(bf16[128,1024]{1,0:T(8,128)(2,1)} %x_hbm.1) | copy-start | bytes 786436
  4.9 0.9 %copy-start.4 = (bf16[1024,128]{1,0:T(8,128)(2,1)S(1)}, bf16[1024,128]{1,0:T(8,128)(2,1)}, u32[]{:S(2)}) copy-start(bf16[1024,128]{1,0:T(8,128)(2,1)} %wq_hbm.1) | copy-start | bytes 786436
  5.8 0.9 %copy-start.5 = (bf16[1024,128]{1,0:T(8,128)(2,1)S(1)}, bf16[1024,128]{1,0:T(8,128)(2,1)}, u32[]{:S(2)}) copy-start(bf16[1024,128]{1,0:T(8,128)(2,1)} %wk_hbm.1) | copy-start | bytes 786436
  6.8 0.9 %copy-start.6 = (bf16[1024,128]{1,0:T(8,128)(2,1)S(1)}, bf16[1024,128]{1,0:T(8,128)(2,1)}, u32[]{:S(2)}) copy-start(bf16[1024,128]{1,0:T(8,128)(2,1)} %wv_hbm.1) | copy-start | bytes 786436
  7.8 0.9 %copy-start.7 = (bf16[128,1024]{1,0:T(8,128)(2,1)S(1)}, bf16[128,1024]{1,0:T(8,128)(2,1)}, u32[]{:S(2)}) copy-start(bf16[128,1024]{1,0:T(8,128)(2,1)} %wo_hbm.1) | copy-start | bytes 786436

commit v2 on v1

v2 whole, which is shorter than its diff:
```python
import jax
import jax.numpy as jnp
from jax import lax
from jax.experimental import pallas as pl
from jax.experimental.pallas import tpu as pltpu
from jax.sharding import PartitionSpec as P

DH = 64
EPS = 1e-06
NEG = -1e30
FLOOR = -1e29
MESH = pl.DeviceIdType.MESH
F32 = jnp.float32
BF16 = jnp.bfloat16


def dot(a, b):
    return jnp.dot(a, b, preferred_element_type=F32)


def dot_nt(a, b):
    return lax.dot_general(a, b, (((1,), (1,)), ((), ())), preferred_element_type=F32)


def norm(states, gain):
    mean_square = jnp.mean(states * states, axis=-1, keepdims=True)
    return (states * lax.rsqrt(mean_square + EPS) * gain).astype(BF16)


def kernel(
    ids_ref, x_hbm, seg_hbm, pk_hbm, pv_hbm, creq_hbm, emb_hbm,
    ag_hbm, fg_hbm, lg_hbm, wq_hbm, wk_hbm, wv_hbm, wo_hbm, wg_hbm, wu_hbm, wd_hbm, lm_hbm,
    out_ref, logits_ref, relk_ref, relv_ref,
    x_v, ag_v, fg_v, lg_v, qkv_v, wo_v, ffn_v, lm_v, emb_v, pv_v,
    vrow, kid_s, s_s, p_s, osend, stsend, part_s, nbuf, decp_s, fin_s,
    past, new, idall, qbuf, obuf, stbuf, dbuf, e1buf, e2buf, e3buf,
    rs1buf, ar1buf, rs2buf, ar2buf,
    lsem, ssem, rsem,
):
    c = lax.axis_index("ctx")
    t = lax.axis_index("tp")
    y = lax.div(c, 4)
    zc = lax.rem(c, 4)

    def ypeer(d):
        return (lax.rem(y + d, 4) * 4 + zc, t)

    def zpeer(e):
        return (y * 4 + lax.rem(zc + e, 4), t)

    def tpeer(r):
        return (c, lax.rem(t + r, 8))

    names = (
        "past", "new", "ids", "q", "e1", "e2", "e3", "relk", "relv", "part", "stats", "dpart",
        "rs1", "ar1", "ag1", "rs2", "ar2", "ag2",
    )

    def remote(name, src, dst, peer):
        at = names.index(name)
        return pltpu.make_async_remote_copy(
            src_ref=src, dst_ref=dst, send_sem=ssem.at[at], recv_sem=rsem.at[at],
            device_id=peer, device_id_type=MESH,
        )

    def arrived(name, whole):
        remote(name, whole, whole, tpeer(1)).wait_recv()

    def sent(name, whole):
        remote(name, whole, whole, tpeer(1)).wait_send()

    barrier = pltpu.get_barrier_semaphore()
    for r in range(1, 4):
        pl.semaphore_signal(barrier, 1, device_id=ypeer(r), device_id_type=MESH)
    for r in range(1, 4):
        pl.semaphore_signal(barrier, 1, device_id=zpeer(r), device_id_type=MESH)
    for r in range(1, 8):
        pl.semaphore_signal(barrier, 1, device_id=tpeer(r), device_id_type=MESH)

    loads = {}
    todo = [
        ("x", x_hbm, x_v), ("ag", ag_hbm, ag_v),
        ("wk", wk_hbm, qkv_v.at[1]), ("wv", wv_hbm, qkv_v.at[2]), ("wq", wq_hbm, qkv_v.at[0]),
        ("pk", pk_hbm, past.at[0, pl.ds(0, 128)]), ("pv", pv_hbm, pv_v),
        ("seg", seg_hbm, idall.at[0, 0]), ("creq", creq_hbm, idall.at[0, 1]),
        ("emb", emb_hbm, emb_v), ("wo", wo_hbm, wo_v), ("fg", fg_hbm, fg_v),
        ("wg", wg_hbm, ffn_v.at[0]), ("wu", wu_hbm, ffn_v.at[1]), ("wd", wd_hbm, ffn_v.at[2]),
        ("lg", lg_hbm, lg_v), ("lm", lm_hbm, lm_v),
    ]
    for i, (name, src, dst) in enumerate(todo):
        loads[name] = pltpu.make_async_copy(src, dst, lsem.at[i])
        loads[name].start()

    def gain_of(ref):
        return ref[...].astype(F32).reshape(1, 1024)

    loads["x"].wait()
    loads["ag"].wait()
    a_gain = gain_of(ag_v)
    normed = norm(x_v[...].astype(F32), a_gain)
    loads["wk"].wait()
    new[0, 0:128, :] = dot(normed, qkv_v[1]).astype(BF16)
    loads["wv"].wait()
    values = dot(normed, qkv_v[2])
    vrow[...] = values.astype(BF16)
    new[0, 128:256, :] = values.T.astype(BF16)
    loads["wq"].wait()
    queries = dot(normed, qkv_v[0]).astype(BF16).astype(F32) * 0.125
    qbuf[0] = queries.T.astype(BF16)
    loads["pk"].wait()
    loads["pv"].wait()
    past[0, 128:256, :] = pv_v[...].astype(F32).T.astype(BF16)
    loads["seg"].wait()
    loads["creq"].wait()

    pl.semaphore_wait(barrier, 13)

    for d in range(1, 4):
        remote("new", new.at[0], new.at[d], ypeer(d)).start()
    for e in range(1, 4):
        remote("q", qbuf.at[0], qbuf.at[e], zpeer(e)).start()
    for d in range(1, 4):
        remote("past", past.at[0], past.at[d], ypeer(d)).start()
    for d in range(1, 4):
        remote("ids", idall.at[0], idall.at[d], ypeer(d)).start()
        remote("ids", idall.at[0], idall.at[3 + d], zpeer(d)).start()

    first_row = (c * 8 + t) * 251
    row16 = lax.broadcasted_iota(jnp.int32, (16, 251), 0)
    col16 = lax.broadcasted_iota(jnp.int32, (16, 251), 1) + first_row
    wanted = jnp.full((16, 251), -1, jnp.int32)
    for q in range(4):
        wanted = jnp.where(row16 == q, ids_ref[q], wanted)
    one_hot = (col16 == wanted).astype(F32).astype(BF16)
    loads["emb"].wait()
    e1buf[0] = dot(one_hot, emb_v[...])[0:4].astype(BF16)
    for d in range(1, 4):
        remote("e1", e1buf.at[0], e1buf.at[d], ypeer(d)).start()

    my_columns = pl.ds(pl.multiple_of(t * 128, 128), 128)
    my_rows = pl.ds(pl.multiple_of(t * 16, 16), 16)

    def rows_of(r):
        return pl.ds(pl.multiple_of(lax.rem(t + r, 8) * 16, 16), 16)

    for r in range(1, 8):
        remote("relk", new.at[0, rows_of(r)], relk_ref.at[:, my_columns], tpeer(r)).start()
        remote("relv", vrow.at[rows_of(r)], relv_ref.at[:, my_columns], tpeer(r)).start()
    relk_ref[:, my_columns] = new[0, my_rows, :]
    relv_ref[:, my_columns] = vrow[my_rows, :]

    arrived("ids", idall.at[pl.ds(1, 6)])
    id_rows = [idall[d, 0:1, :].astype(F32) for d in range(4)]
    id_rows += [idall[d, 1:2, :].astype(F32) for d in range(4)]
    id_columns = jnp.concatenate(id_rows + [jnp.zeros((120, 128), F32)], axis=0).T
    for b in range(8):
        kid_s[b] = jnp.broadcast_to(id_columns[:, b : b + 1], (128, 128))
    idall[7] = idall[0]
    arrived("q", qbuf.at[pl.ds(1, 3)])
    arrived("new", new.at[pl.ds(1, 3)])
    arrived("past", past.at[pl.ds(1, 3)])

    def block(b):
        return new.at[b] if b < 4 else past.at[b - 4]

    arrived("e1", e1buf.at[pl.ds(1, 3)])
    e2buf[0] = sum(e1buf[d].astype(F32) for d in range(4)).astype(BF16)
    for e in range(1, 4):
        remote("e2", e2buf.at[0], e2buf.at[e], zpeer(e)).start()

    k_iota = lax.broadcasted_iota(jnp.int32, (128, 128), 0)
    q_iota = lax.broadcasted_iota(jnp.int32, (128, 128), 1)

    def attend(i, _):
        e = lax.rem(i + 1, 4)
        qt = qbuf[e]
        top = qt[0:64, :]
        low = qt[64:128, :]
        zero = jnp.zeros((64, 128), BF16)
        qd = jnp.concatenate(
            [jnp.concatenate([top, zero], axis=1), jnp.concatenate([zero, low], axis=1)], axis=0)
        qid = idall[4 + lax.rem(e + 3, 4), 0:1, :].astype(F32)
        q_at = y * 512 + lax.rem(zc - e + 4, 4) * 128
        highest = jnp.full((8, 256), FLOOR, F32)
        for b in range(8):
            s = dot(block(b)[0:128, :], qd)
            ok = kid_s[b] == qid
            if b < 4:
                k_at = lax.rem(y - b + 4, 4) * 512 + zc * 128
                ok = ok & (k_iota + (k_at - q_at) <= q_iota)
            s = jnp.where(jnp.concatenate([ok, ok], axis=1), s, NEG)
            s_s[b * 128 : (b + 1) * 128, :] = s
            highest = jnp.maximum(highest, jnp.max(s.reshape(16, 8, 256), axis=0))
        m = jnp.max(highest, axis=0, keepdims=True)
        total_w = jnp.zeros((8, 256), F32)
        o = jnp.zeros((128, 256), F32)
        for b in range(8):
            w = jnp.exp(s_s[b * 128 : (b + 1) * 128, :] - m)
            total_w = total_w + jnp.sum(w.reshape(16, 8, 256), axis=0)
            o = o + dot(block(b)[128:256, :], w.astype(BF16))
        l = jnp.sum(total_w, axis=0, keepdims=True)
        f = lax.rem(4 - e, 4)
        osend[f] = jnp.concatenate([o[0:64, 0:128], o[64:128, 128:256]], axis=0).astype(BF16)
        stsend[f] = jnp.concatenate(
            [m[:, 0:128], m[:, 128:256], l[:, 0:128], l[:, 128:256], jnp.zeros((4, 128), F32)],
            axis=0)

        @pl.when(i < 3)
        def _():
            remote("part", osend.at[f], obuf.at[f], zpeer(f)).start()
            remote("stats", stsend.at[f], stbuf.at[f], zpeer(f)).start()

        return 0

    lax.fori_loop(0, 4, attend, 0)
    obuf[0] = osend[0]
    stbuf[0] = stsend[0]

    arrived("e2", e2buf.at[pl.ds(1, 3)])
    e3buf[0] = sum(e2buf[e].astype(F32) for e in range(4)).astype(BF16)
    for r in range(1, 8):
        remote("e3", e3buf.at[0], e3buf.at[r], tpeer(r)).start()

    arrived("part", obuf.at[pl.ds(1, 3)])
    arrived("stats", stbuf.at[pl.ds(1, 3)])
    stats = [stbuf[f] for f in range(4)]
    tops = [st[0:2] for st in stats]
    joint = jnp.maximum(jnp.maximum(tops[0], tops[1]), jnp.maximum(tops[2], tops[3]))
    scales = [jnp.exp(m - joint) for m in tops]
    weight = sum(sc * st[2:4] for sc, st in zip(scales, stats))
    inverse = 1.0 / weight
    attended = jnp.zeros((128, 128), F32)
    for f in range(4):
        factor = scales[f] * inverse
        spread = jnp.concatenate(
            [jnp.broadcast_to(factor[0:1], (64, 128)), jnp.broadcast_to(factor[1:2], (64, 128))],
            axis=0)
        attended = attended + obuf[f].astype(F32) * spread
    loads["wo"].wait()
    head_term = dot(attended.T.astype(BF16), wo_v[...])
    part_s[0] = head_term.astype(BF16)
    for r in range(1, 8):
        remote("rs1", part_s.at[0, rows_of(r)], rs1buf.at[r], tpeer(r)).start()

    arrived("e3", e3buf.at[pl.ds(1, 7)])
    embedded = sum(e3buf[r].astype(F32) for r in range(8))

    def padded(rows):
        return jnp.concatenate([rows, jnp.zeros((12,) + rows.shape[1:], F32)], axis=0).astype(BF16)

    d_normed = padded(norm(embedded, a_gain).astype(F32))
    dq = dot(d_normed, qkv_v[0]).astype(BF16).astype(F32)[0:4] * 0.125
    dk = dot(d_normed, qkv_v[1]).astype(BF16).astype(F32)[0:4]
    dv = dot(d_normed, qkv_v[2]).astype(BF16).astype(F32)[0:4]
    lane4 = lax.broadcasted_iota(jnp.int32, (4, 128), 1)
    qd8 = jnp.concatenate(
        [jnp.where(lane4 < 64, dq, 0.0), jnp.where(lane4 >= 64, dq, 0.0)], axis=0)
    qd16 = jnp.concatenate([qd8, jnp.zeros((8, 128), F32)], axis=0).astype(BF16)
    k_ids = jnp.concatenate(id_rows, axis=1)
    rid = (lax.broadcasted_iota(jnp.int32, (16, 1024), 0) % 4).astype(F32)
    s = jnp.concatenate([dot_nt(qd16, block(b)[0:128, :]) for b in range(8)], axis=1)
    s = jnp.where(rid == k_ids, s, NEG)
    m = jnp.maximum(jnp.max(s, axis=1, keepdims=True), FLOOR)
    w = jnp.exp(s - m)
    l = jnp.sum(w, axis=1, keepdims=True)
    w = w.astype(BF16)
    o = sum(
        dot_nt(w[:, b * 128 : (b + 1) * 128], block(b)[128:256, :]) for b in range(8))
    dbuf[0, 0:8, :] = o[0:8]
    dbuf[0, 8:16, :] = jnp.broadcast_to(m[0:8], (8, 128))
    dbuf[0, 16:24, :] = jnp.broadcast_to(l[0:8], (8, 128))
    for e in range(1, 4):
        remote("dpart", dbuf.at[0], dbuf.at[e], zpeer(e)).start()

    residual = x_v[my_rows, :].astype(F32) + part_s[0, my_rows, :].astype(F32)
    arrived("rs1", rs1buf.at[pl.ds(1, 7)])
    for r in range(1, 8):
        residual = residual + rs1buf[r].astype(F32)
    loads["fg"].wait()
    f_gain = gain_of(fg_v)
    nbuf[my_rows, :] = norm(residual, f_gain)
    for r in range(1, 8):
        remote("ag1", nbuf.at[my_rows], nbuf.at[my_rows], tpeer(r)).start()
    fin_s[...] = residual

    own_m = jnp.sum(qd8 * jnp.concatenate([dk, dk], axis=0), axis=1, keepdims=True)
    own_m = jnp.broadcast_to(own_m, (8, 128))
    arrived("dpart", dbuf.at[pl.ds(1, 3)])
    dparts = [dbuf[e] for e in range(4)]
    joint = own_m
    for part in dparts:
        joint = jnp.maximum(joint, part[8:16])
    own_scale = jnp.exp(own_m - joint)
    weight = own_scale
    summed = own_scale * jnp.concatenate([dv, dv], axis=0)
    for part in dparts:
        scale = jnp.exp(part[8:16] - joint)
        weight = weight + scale * part[16:24]
        summed = summed + scale * part[0:8]
    summed = summed / weight
    d_attended = padded(jnp.where(lane4 < 64, summed[0:4], summed[4:8]))
    ar1buf[0] = dot(d_attended, wo_v[...])[0:4].astype(BF16)
    for r in range(1, 8):
        remote("ar1", ar1buf.at[0], ar1buf.at[r], tpeer(r)).start()

    def units(rows):
        gate = dot_nt(rows, ffn_v[0])
        up = dot_nt(rows, ffn_v[1])
        hidden = (jax.nn.gelu(gate, approximate=True) * up).astype(BF16)
        return dot(hidden, ffn_v[2])

    loads["wg"].wait()
    loads["wu"].wait()
    loads["wd"].wait()
    arrived("ag1", nbuf.at[pl.ds(0, 112)])
    part_s[1] = units(nbuf[...]).astype(BF16)
    for r in range(1, 8):
        remote("rs2", part_s.at[1, rows_of(r)], rs2buf.at[r], tpeer(r)).start()

    arrived("ar1", ar1buf.at[pl.ds(1, 7)])
    d_residual = embedded + sum(ar1buf[r].astype(F32) for r in range(8))
    ar2buf[0] = units(padded(norm(d_residual, f_gain).astype(F32)))[0:4].astype(BF16)
    for r in range(1, 8):
        remote("ar2", ar2buf.at[0], ar2buf.at[r], tpeer(r)).start()

    final = fin_s[...] + part_s[1, my_rows, :].astype(F32)
    arrived("rs2", rs2buf.at[pl.ds(1, 7)])
    for r in range(1, 8):
        final = final + rs2buf[r].astype(F32)
    out_ref[my_rows, :] = final.astype(BF16)
    for r in range(1, 8):
        remote("ag2", out_ref.at[my_rows], out_ref.at[my_rows], tpeer(r)).start()

    arrived("ar2", ar2buf.at[pl.ds(1, 7)])
    d_final = d_residual + sum(ar2buf[r].astype(F32) for r in range(8))
    loads["lg"].wait()
    loads["lm"].wait()
    l_normed = padded(norm(d_final, gain_of(lg_v)).astype(F32))
    logits_ref[...] = dot(l_normed, lm_v[...])[0:4]

    arrived("relk", relk_ref.at[:, pl.ds(0, 896)])
    arrived("relv", relv_ref.at[:, pl.ds(0, 896)])
    sent("new", new.at[pl.ds(1, 3)])
    sent("past", past.at[pl.ds(1, 3)])
    sent("ids", idall.at[pl.ds(1, 6)])
    sent("q", qbuf.at[pl.ds(1, 3)])
    sent("e1", e1buf.at[pl.ds(1, 3)])
    sent("e2", e2buf.at[pl.ds(1, 3)])
    sent("e3", e3buf.at[pl.ds(1, 7)])
    sent("relk", relk_ref.at[:, pl.ds(0, 896)])
    sent("relv", relv_ref.at[:, pl.ds(0, 896)])
    sent("part", obuf.at[pl.ds(1, 3)])
    sent("stats", stbuf.at[pl.ds(1, 3)])
    sent("dpart", dbuf.at[pl.ds(1, 3)])
    sent("rs1", rs1buf.at[pl.ds(1, 7)])
    sent("ar1", ar1buf.at[pl.ds(1, 7)])
    sent("ag1", nbuf.at[pl.ds(0, 112)])
    sent("rs2", rs2buf.at[pl.ds(1, 7)])
    sent("ar2", ar2buf.at[pl.ds(1, 7)])
    arrived("ag2", out_ref.at[pl.ds(0, 112)])
    sent("ag2", out_ref.at[pl.ds(0, 112)])


def hand_over(*refs):
    sems = refs[8]
    copies = [pltpu.make_async_copy(refs[i], refs[4 + i], sems.at[i]) for i in range(4)]
    for copy in copies:
        copy.start()
    for copy in copies:
        copy.wait()


def on_device(
    prompt_states, segment_ids, past_keys, past_values, cache_request, decode_ids, embed_table,
    attn_gain, ff_gain, final_gain, w_query, w_key, w_value, w_out, w_gate, w_up, w_down, lm_head,
):
    in_hbm = pl.BlockSpec(memory_space=pltpu.HBM)
    in_vmem = pl.BlockSpec(memory_space=pltpu.VMEM)
    dma = pltpu.SemaphoreType.DMA
    local = [
        ((128, 1024), BF16), ((1024,), BF16), ((1024,), BF16), ((1024,), BF16),
        ((3, 1024, 128), BF16), ((128, 1024), BF16), ((3, 352, 1024), BF16), ((1024, 251), BF16),
        ((251, 1024), BF16), ((128, 128), BF16),
        ((128, 128), BF16), ((8, 128, 128), F32), ((1024, 256), F32), ((8, 128), BF16),
        ((4, 128, 128), BF16), ((4, 8, 128), F32), ((2, 128, 1024), BF16), ((128, 1024), BF16),
        ((8, 128), BF16), ((16, 1024), F32),
    ]
    arriving = [
        ((4, 256, 128), BF16), ((4, 256, 128), BF16), ((8, 8, 128), jnp.int32),
        ((4, 128, 128), BF16), ((4, 128, 128), BF16), ((4, 8, 128), F32), ((4, 24, 128), F32),
        ((4, 4, 1024), BF16), ((4, 4, 1024), BF16), ((8, 4, 1024), BF16),
        ((8, 16, 1024), BF16), ((8, 4, 1024), BF16), ((8, 16, 1024), BF16), ((8, 4, 1024), BF16),
    ]
    shapes = [((128, 1024), BF16), ((4, 251), F32), ((16, 1024), BF16), ((16, 1024), BF16)]
    arrays = [
        pltpu.with_memory_space_constraint(a, pltpu.HBM)
        for a in (
            prompt_states, segment_ids, past_keys, past_values, cache_request, embed_table,
            attn_gain, ff_gain, final_gain, w_query, w_key, w_value, w_out, w_gate.T, w_up.T,
            w_down, lm_head,
        )
    ]
    results = pl.pallas_call(
        kernel,
        out_shape=tuple(pltpu.VMEM(s, d) for s, d in shapes),
        in_specs=[pl.BlockSpec(memory_space=pltpu.SMEM)] + [in_hbm] * 17,
        out_specs=(in_vmem,) * 4,
        scratch_shapes=[pltpu.VMEM(s, d) for s, d in local + arriving]
        + [dma((17,)), dma((18,)), dma((18,))],
        compiler_params=pltpu.CompilerParams(
            collective_id=0, has_side_effects=True, vmem_limit_bytes=60 * 1024 * 1024),
    )(decode_ids, *arrays)
    results = [pltpu.with_memory_space_constraint(a, pltpu.VMEM) for a in results]
    return pl.pallas_call(
        hand_over,
        out_shape=tuple(jax.ShapeDtypeStruct(s, d) for s, d in shapes),
        in_specs=[in_vmem] * 4,
        out_specs=(in_hbm,) * 4,
        scratch_shapes=[dma((4,))],
    )(*results)


def solution(mesh):
    placed = (
        P("ctx", None),
        P("ctx"),
        P("ctx", "tp"),
        P("ctx", "tp"),
        P("ctx"),
        P(),
        P(("ctx", "tp"), None),
        P(),
        P(),
        P(),
        P(None, "tp"),
        P(None, "tp"),
        P(None, "tp"),
        P("tp", None),
        P(None, "tp"),
        P(None, "tp"),
        P("tp", None),
        P(None, ("ctx", "tp")),
    )
    return jax.shard_map(
        on_device,
        mesh=mesh,
        in_specs=placed,
        out_specs=(
            P("ctx", None),
            P(None, ("ctx", "tp")),
            P(("ctx", "tp"), None),
            P(("ctx", "tp"), None),
        ),
        check_vma=False,
    )
```

time: 60 us -> 47.8 us (0.80)
  local copies, waits for them, and re-layouts: 10.4 us -> 0 us
  Pallas kernels: 48.2 us -> 47 us
    unnamed x38 -> x0, local copies, waits for them, and re-layouts: 10.4 us -> none
    pallas_call x1 -> x2, Pallas kernels: 48.2 us -> 47 us  [the longest x1 46.3 us: on_device(): pl.pallas_call(kernel, out_shape=tuple((pltpu.VMEM(s, d) for s, d in shap...]
where the time goes in v2:
time: 47.8 us; the launch traced here: 47.7 us
  Pallas kernels  47 us (98%)
  between operations  0.65 us (1%)
    pallas_call x1, Pallas kernels, on_device(): pl.pallas_call(kernel, out_shape=tuple((pltpu.VMEM(s, d) for s, d in shap...  46.3 us

profile of v2, /device:TPU:0, one launch (start us, length us, event | category | flops | bytes accessed | tf_op | source)
XLA Modules:
  0.0 47.7 jit_solution(13221993031522899472)
XLA Ops:
  0.6 46.3 %shard_map.201 = (bf16[128,1024]{1,0:T(8,128)(2,1)S(1)}, f32[4,251]{1,0:T(4,128)S(1)}, bf16[16,1024]{1,0:T(8,128)(2,1)S(1)}, bf16[16,1024]{1,0:T(8,128)(2,1)S(1)}) custom-call(s32[4]{0:T(128)} %ids_ref.1, bf16[128,1024]{1,0:T(8,128)(2,1)} %x_hbm.1, s32[128]{0:T(128)} %seg_hbm.1, bf16[128,128]{1,0:T(8,128)(2,1)} %pk_hbm.1, bf16[128,128]{1,0:T(8,128)(2,1)} %pv_hbm.1, ...), custom_call_target="tpu_custom_call" | custom-call | tf_op jit(solution)/shard_map/pallas_call | solution.py:403
  46.9 0.8 %shard_map.202 = (bf16[128,1024]{1,0:T(8,128)(2,1)}, f32[4,251]{1,0:T(4,128)}, bf16[16,1024]{1,0:T(8,128)(2,1)}, bf16[16,1024]{1,0:T(8,128)(2,1)}) custom-call(bf16[128,1024]{1,0:T(8,128)(2,1)S(1)} %get-tuple-element.8.refs_0_, f32[4,251]{1,0:T(4,128)S(1)} %get-tuple-element.9.refs_1_, bf16[16,1024]{1,0:T(8,128)(2,1)S(1)} %get-tuple-element.10.refs_2_, ...), custom_call_target="tpu_custom_call" | custom-call | tf_op jit(solution)/shard_map/pallas_call | solution.py:414

commit v3 on v2

--- a/solution.py
+++ b/solution.py
@@ -31,29 +31,43 @@
     ids_ref, x_hbm, seg_hbm, pk_hbm, pv_hbm, creq_hbm, emb_hbm,
     ag_hbm, fg_hbm, lg_hbm, wq_hbm, wk_hbm, wv_hbm, wo_hbm, wg_hbm, wu_hbm, wd_hbm, lm_hbm,
     out_ref, logits_ref, relk_ref, relv_ref,
-    x_v, ag_v, fg_v, lg_v, qkv_v, wo_v, ffn_v, lm_v, emb_v, pv_v,
-    vrow, kid_s, s_s, p_s, osend, stsend, part_s, nbuf, decp_s, fin_s,
+    x_v, ag_v, fg_v, lg_v, qkv_v, ffn_v, lm_v, emb_v, pv_v,
+    vrow, kid_s, s_s, hi_s, tw_s, o_s, osend, stsend, part_s, nbuf, res_s,
     past, new, idall, qbuf, obuf, stbuf, dbuf, e1buf, e2buf, e3buf,
-    rs1buf, ar1buf, rs2buf, ar2buf,
+    wo_full, abuf, dabuf, rs2buf, ar2buf,
     lsem, ssem, rsem,
 ):
     c = lax.axis_index("ctx")
     t = lax.axis_index("tp")
     y = lax.div(c, 4)
     zc = lax.rem(c, 4)
+    z_hi = lax.div(zc, 2)
+    core = lax.rem(c, 2)
+    z_lo = lax.div(t, 4)
+    x = lax.rem(t, 4)
 
     def ypeer(d):
         return (lax.rem(y + d, 4) * 4 + zc, t)
 
-    def zpeer(e):
-        return (y * 4 + lax.rem(zc + e, 4), t)
+    def zc_of(g):
+        return lax.rem(z_hi + lax.div(g, 2), 2) * 2 + lax.rem(core + lax.rem(g, 2), 2)
+
+    def zpeer(g):
+        return (y * 4 + zc_of(jnp.int32(g)), t)
+
+    def t_of(r):
+        return lax.rem(z_lo + r // 4, 2) * 4 + lax.rem(x + r % 4, 4)
 
     def tpeer(r):
-        return (c, lax.rem(t + r, 8))
+        return (c, t_of(r))
+
+    y_order = (2, 1, 3)
+    z_order = (3, 2, 1)
+    t_order = (6, 5, 7, 2, 4, 1, 3)
 
     names = (
-        "past", "new", "ids", "q", "e1", "e2", "e3", "relk", "relv", "part", "stats", "dpart",
-        "rs1", "ar1", "ag1", "rs2", "ar2", "ag2",
+        "past", "new1", "new2", "new3", "ids", "q", "e1", "e2", "e3", "relk", "relv",
+        "part", "stats", "dpart", "wo", "woz", "wof", "swap", "att", "datt", "rs2", "ar2", "ag2",
     )
 
     def remote(name, src, dst, peer):
@@ -77,13 +91,14 @@
     for r in range(1, 8):
         pl.semaphore_signal(barrier, 1, device_id=tpeer(r), device_id_type=MESH)
 
+    my_half = pl.ds(pl.multiple_of(core * 64, 64), 64)
     loads = {}
     todo = [
         ("x", x_hbm, x_v), ("ag", ag_hbm, ag_v),
         ("wk", wk_hbm, qkv_v.at[1]), ("wv", wv_hbm, qkv_v.at[2]), ("wq", wq_hbm, qkv_v.at[0]),
         ("pk", pk_hbm, past.at[0, pl.ds(0, 128)]), ("pv", pv_hbm, pv_v),
         ("seg", seg_hbm, idall.at[0, 0]), ("creq", creq_hbm, idall.at[0, 1]),
-        ("emb", emb_hbm, emb_v), ("wo", wo_hbm, wo_v), ("fg", fg_hbm, fg_v),
+        ("emb", emb_hbm, emb_v), ("wo", wo_hbm.at[my_half], wo_full.at[t, core]), ("fg", fg_hbm, fg_v),
         ("wg", wg_hbm, ffn_v.at[0]), ("wu", wu_hbm, ffn_v.at[1]), ("wd", wd_hbm, ffn_v.at[2]),
         ("lg", lg_hbm, lg_v), ("lm", lm_hbm, lm_v),
     ]
@@ -115,15 +130,19 @@
 
     pl.semaphore_wait(barrier, 13)
 
-    for d in range(1, 4):
-        remote("new", new.at[0], new.at[d], ypeer(d)).start()
-    for e in range(1, 4):
-        remote("q", qbuf.at[0], qbuf.at[e], zpeer(e)).start()
-    for d in range(1, 4):
+    def send_new(d):
+        remote("new%d" % d, new.at[0], new.at[d], ypeer(d)).start()
+
+    for d in (2, 1):
+        pl.when(y + d < 4)(lambda d=d: send_new(d))
+    for g in z_order:
+        remote("q", qbuf.at[0], qbuf.at[g], zpeer(g)).start()
+    for d in y_order:
         remote("past", past.at[0], past.at[d], ypeer(d)).start()
-    for d in range(1, 4):
+    for d in y_order:
         remote("ids", idall.at[0], idall.at[d], ypeer(d)).start()
-        remote("ids", idall.at[0], idall.at[3 + d], zpeer(d)).start()
+    for g in z_order:
+        remote("ids", idall.at[0], idall.at[3 + g], zpeer(g)).start()
 
     first_row = (c * 8 + t) * 251
     row16 = lax.broadcasted_iota(jnp.int32, (16, 251), 0)
@@ -134,81 +153,122 @@
     one_hot = (col16 == wanted).astype(F32).astype(BF16)
     loads["emb"].wait()
     e1buf[0] = dot(one_hot, emb_v[...])[0:4].astype(BF16)
-    for d in range(1, 4):
-        remote("e1", e1buf.at[0], e1buf.at[d], ypeer(d)).start()
+    for r in t_order:
+        remote("e1", e1buf.at[0], e1buf.at[r], tpeer(r)).start()
+
+    remote("woz", wo_hbm.at[my_half], wo_full.at[t, core], tpeer(4)).start()
+    for r in (2, 1, 3):
+        remote("wo", wo_hbm.at[my_half], wo_full.at[t, core], tpeer(r)).start()
 
     my_columns = pl.ds(pl.multiple_of(t * 128, 128), 128)
     my_rows = pl.ds(pl.multiple_of(t * 16, 16), 16)
 
     def rows_of(r):
-        return pl.ds(pl.multiple_of(lax.rem(t + r, 8) * 16, 16), 16)
-
-    for r in range(1, 8):
+        return pl.ds(pl.multiple_of(t_of(r) * 16, 16), 16)
+
+    for d in (2, 1):
+        pl.when(y + d >= 4)(lambda d=d: send_new(d))
+    send_new(3)
+    for r in t_order:
         remote("relk", new.at[0, rows_of(r)], relk_ref.at[:, my_columns], tpeer(r)).start()
         remote("relv", vrow.at[rows_of(r)], relv_ref.at[:, my_columns], tpeer(r)).start()
     relk_ref[:, my_columns] = new[0, my_rows, :]
     relv_ref[:, my_columns] = vrow[my_rows, :]
 
+    arrived("woz", wo_full.at[0, 0])
+    across = t_of(4)
+    for r in (2, 1, 3):
+        remote("wof", wo_full.at[across, core], wo_full.at[across, core], tpeer(r)).start()
+
+    arrived("e1", e1buf.at[pl.ds(1, 7)])
+    e2buf[0] = sum(e1buf[r].astype(F32) for r in range(8)).astype(BF16)
+    for g in z_order:
+        remote("e2", e2buf.at[0], e2buf.at[g], zpeer(g)).start()
+
     arrived("ids", idall.at[pl.ds(1, 6)])
-    id_rows = [idall[d, 0:1, :].astype(F32) for d in range(4)]
-    id_rows += [idall[d, 1:2, :].astype(F32) for d in range(4)]
-    id_columns = jnp.concatenate(id_rows + [jnp.zeros((120, 128), F32)], axis=0).T
+    new_ids = [idall[d, 0:1, :].astype(F32) for d in range(4)]
+    past_ids = [idall[d, 1:2, :].astype(F32) for d in range(4)]
+    id_columns = jnp.concatenate(
+        new_ids + past_ids + [jnp.zeros((120, 128), F32)], axis=0).T
     for b in range(8):
         kid_s[b] = jnp.broadcast_to(id_columns[:, b : b + 1], (128, 128))
     idall[7] = idall[0]
     arrived("q", qbuf.at[pl.ds(1, 3)])
-    arrived("new", new.at[pl.ds(1, 3)])
+    pl.when(y >= 1)(lambda: arrived("new1", new.at[1]))
+    pl.when(y >= 2)(lambda: arrived("new2", new.at[2]))
     arrived("past", past.at[pl.ds(1, 3)])
 
     def block(b):
         return new.at[b] if b < 4 else past.at[b - 4]
 
-    arrived("e1", e1buf.at[pl.ds(1, 3)])
-    e2buf[0] = sum(e1buf[d].astype(F32) for d in range(4)).astype(BF16)
-    for e in range(1, 4):
-        remote("e2", e2buf.at[0], e2buf.at[e], zpeer(e)).start()
-
     k_iota = lax.broadcasted_iota(jnp.int32, (128, 128), 0)
     q_iota = lax.broadcasted_iota(jnp.int32, (128, 128), 1)
 
     def attend(i, _):
-        e = lax.rem(i + 1, 4)
-        qt = qbuf[e]
+        g = 3 - i
+        qt = qbuf[g]
         top = qt[0:64, :]
         low = qt[64:128, :]
         zero = jnp.zeros((64, 128), BF16)
         qd = jnp.concatenate(
             [jnp.concatenate([top, zero], axis=1), jnp.concatenate([zero, low], axis=1)], axis=0)
-        qid = idall[4 + lax.rem(e + 3, 4), 0:1, :].astype(F32)
-        q_at = y * 512 + lax.rem(zc - e + 4, 4) * 128
-        highest = jnp.full((8, 256), FLOOR, F32)
-        for b in range(8):
+        qid = idall[4 + lax.rem(g + 3, 4), 0:1, :].astype(F32)
+        q_at = y * 512 + zc_of(g) * 128
+
+        def score(b):
             s = dot(block(b)[0:128, :], qd)
             ok = kid_s[b] == qid
             if b < 4:
-                k_at = lax.rem(y - b + 4, 4) * 512 + zc * 128
+                k_at = (y - b) * 512 + zc * 128
                 ok = ok & (k_iota + (k_at - q_at) <= q_iota)
             s = jnp.where(jnp.concatenate([ok, ok], axis=1), s, NEG)
             s_s[b * 128 : (b + 1) * 128, :] = s
-            highest = jnp.maximum(highest, jnp.max(s.reshape(16, 8, 256), axis=0))
-        m = jnp.max(highest, axis=0, keepdims=True)
+            return jnp.max(s.reshape(16, 8, 256), axis=0)
+
+        def weigh(b, m):
+            w = jnp.exp(s_s[b * 128 : (b + 1) * 128, :] - m)
+            return jnp.sum(w.reshape(16, 8, 256), axis=0), dot(
+                block(b)[128:256, :], w.astype(BF16))
+
+        always = (0, 4, 5, 6, 7)
+        highest = jnp.full((8, 256), FLOOR, F32)
+        for b in always:
+            highest = jnp.maximum(highest, score(b))
+        hi_s[...] = highest
+
+        def score_more(b):
+            hi_s[...] = jnp.maximum(hi_s[...], score(b))
+
+        pl.when(y >= 1)(lambda: score_more(1))
+        pl.when(y >= 2)(lambda: score_more(2))
+        m = jnp.max(hi_s[...], axis=0, keepdims=True)
         total_w = jnp.zeros((8, 256), F32)
         o = jnp.zeros((128, 256), F32)
-        for b in range(8):
-            w = jnp.exp(s_s[b * 128 : (b + 1) * 128, :] - m)
-            total_w = total_w + jnp.sum(w.reshape(16, 8, 256), axis=0)
-            o = o + dot(block(b)[128:256, :], w.astype(BF16))
-        l = jnp.sum(total_w, axis=0, keepdims=True)
-        f = lax.rem(4 - e, 4)
-        osend[f] = jnp.concatenate([o[0:64, 0:128], o[64:128, 128:256]], axis=0).astype(BF16)
-        stsend[f] = jnp.concatenate(
+        for b in always:
+            more_w, more_o = weigh(b, m)
+            total_w = total_w + more_w
+            o = o + more_o
+        tw_s[...] = total_w
+        o_s[...] = o
+
+        def weigh_more(b):
+            more_w, more_o = weigh(b, m)
+            tw_s[...] += more_w
+            o_s[...] += more_o
+
+        pl.when(y >= 1)(lambda: weigh_more(1))
+        pl.when(y >= 2)(lambda: weigh_more(2))
+        l = jnp.sum(tw_s[...], axis=0, keepdims=True)
+        osend[g] = jnp.concatenate(
+            [o_s[0:64, 0:128], o_s[64:128, 128:256]], axis=0).astype(BF16)
+        stsend[g] = jnp.concatenate(
             [m[:, 0:128], m[:, 128:256], l[:, 0:128], l[:, 128:256], jnp.zeros((4, 128), F32)],
             axis=0)
 
         @pl.when(i < 3)
         def _():
-            remote("part", osend.at[f], obuf.at[f], zpeer(f)).start()
-            remote("stats", stsend.at[f], stbuf.at[f], zpeer(f)).start()
+            remote("part", osend.at[g], obuf.at[g], zpeer(g)).start()
+            remote("stats", stsend.at[g], stbuf.at[g], zpeer(g)).start()
 
         return 0
 
@@ -217,9 +277,9 @@
     stbuf[0] = stsend[0]
 
     arrived("e2", e2buf.at[pl.ds(1, 3)])
-    e3buf[0] = sum(e2buf[e].astype(F32) for e in range(4)).astype(BF16)
-    for r in range(1, 8):
-        remote("e3", e3buf.at[0], e3buf.at[r], tpeer(r)).start()
+    e3buf[0] = sum(e2buf[g].astype(F32) for g in range(4)).astype(BF16)
+    for d in y_order:
+        remote("e3", e3buf.at[0], e3buf.at[d], ypeer(d)).start()
 
     arrived("part", obuf.at[pl.ds(1, 3)])
     arrived("stats", stbuf.at[pl.ds(1, 3)])
@@ -236,14 +296,20 @@
             [jnp.broadcast_to(factor[0:1], (64, 128)), jnp.broadcast_to(factor[1:2], (64, 128))],
             axis=0)
         attended = attended + obuf[f].astype(F32) * spread
+    abuf[:, my_columns] = attended.T.astype(BF16)
+    for r in t_order:
+        remote("att", abuf.at[:, my_columns], abuf.at[:, my_columns], tpeer(r)).start()
+
+    arrived("wo", wo_full.at[pl.ds(0, 3), 0])
+    arrived("wof", wo_full.at[pl.ds(0, 3), 0])
     loads["wo"].wait()
-    head_term = dot(attended.T.astype(BF16), wo_v[...])
-    part_s[0] = head_term.astype(BF16)
-    for r in range(1, 8):
-        remote("rs1", part_s.at[0, rows_of(r)], rs1buf.at[r], tpeer(r)).start()
-
-    arrived("e3", e3buf.at[pl.ds(1, 7)])
-    embedded = sum(e3buf[r].astype(F32) for r in range(8))
+    remote("swap", wo_full.at[:, core], wo_full.at[:, core], zpeer(1)).start()
+
+    arrived("e3", e3buf.at[pl.ds(1, 3)])
+    embedded = sum(e3buf[d].astype(F32) for d in range(4))
+    pl.when(y < 1)(lambda: arrived("new1", new.at[1]))
+    pl.when(y < 2)(lambda: arrived("new2", new.at[2]))
+    arrived("new3", new.at[3])
 
     def padded(rows):
         return jnp.concatenate([rows, jnp.zeros((12,) + rows.shape[1:], F32)], axis=0).astype(BF16)
@@ -256,7 +322,7 @@
     qd8 = jnp.concatenate(
         [jnp.where(lane4 < 64, dq, 0.0), jnp.where(lane4 >= 64, dq, 0.0)], axis=0)
     qd16 = jnp.concatenate([qd8, jnp.zeros((8, 128), F32)], axis=0).astype(BF16)
-    k_ids = jnp.concatenate(id_rows, axis=1)
+    k_ids = jnp.concatenate(new_ids + past_ids, axis=1)
     rid = (lax.broadcasted_iota(jnp.int32, (16, 1024), 0) % 4).astype(F32)
     s = jnp.concatenate([dot_nt(qd16, block(b)[0:128, :]) for b in range(8)], axis=1)
     s = jnp.where(rid == k_ids, s, NEG)
@@ -269,19 +335,8 @@
     dbuf[0, 0:8, :] = o[0:8]
     dbuf[0, 8:16, :] = jnp.broadcast_to(m[0:8], (8, 128))
     dbuf[0, 16:24, :] = jnp.broadcast_to(l[0:8], (8, 128))
-    for e in range(1, 4):
-        remote("dpart", dbuf.at[0], dbuf.at[e], zpeer(e)).start()
-
-    residual = x_v[my_rows, :].astype(F32) + part_s[0, my_rows, :].astype(F32)
-    arrived("rs1", rs1buf.at[pl.ds(1, 7)])
-    for r in range(1, 8):
-        residual = residual + rs1buf[r].astype(F32)
-    loads["fg"].wait()
-    f_gain = gain_of(fg_v)
-    nbuf[my_rows, :] = norm(residual, f_gain)
-    for r in range(1, 8):
-        remote("ag1", nbuf.at[my_rows], nbuf.at[my_rows], tpeer(r)).start()
-    fin_s[...] = residual
+    for g in z_order:
+        remote("dpart", dbuf.at[0], dbuf.at[g], zpeer(g)).start()
 
     own_m = jnp.sum(qd8 * jnp.concatenate([dk, dk], axis=0), axis=1, keepdims=True)
     own_m = jnp.broadcast_to(own_m, (8, 128))
@@ -298,10 +353,10 @@
         weight = weight + scale * part[16:24]
         summed = summed + scale * part[0:8]
     summed = summed / weight
-    d_attended = padded(jnp.where(lane4 < 64, summed[0:4], summed[4:8]))
-    ar1buf[0] = dot(d_attended, wo_v[...])[0:4].astype(BF16)
-    for r in range(1, 8):
-        remote("ar1", ar1buf.at[0], ar1buf.at[r], tpeer(r)).start()
+    d_attended = jnp.where(lane4 < 64, summed[0:4], summed[4:8])
+    dabuf[t] = d_attended.astype(BF16)
+    for r in t_order:
+        remote("datt", dabuf.at[t], dabuf.at[t], tpeer(r)).start()
 
     def units(rows):
         gate = dot_nt(rows, ffn_v[0])
@@ -309,26 +364,33 @@
         hidden = (jax.nn.gelu(gate, approximate=True) * up).astype(BF16)
         return dot(hidden, ffn_v[2])
 
+    arrived("swap", wo_full.at[:, 0])
+    arrived("att", abuf.at[:, pl.ds(0, 896)])
+    residual = x_v[...].astype(F32) + dot(abuf[...], wo_full[...].reshape(1024, 1024))
+    res_s[...] = residual
+    loads["fg"].wait()
+    f_gain = gain_of(fg_v)
+    nbuf[...] = norm(residual, f_gain)
     loads["wg"].wait()
     loads["wu"].wait()
     loads["wd"].wait()
-    arrived("ag1", nbuf.at[pl.ds(0, 112)])
-    part_s[1] = units(nbuf[...]).astype(BF16)
-    for r in range(1, 8):
-        remote("rs2", part_s.at[1, rows_of(r)], rs2buf.at[r], tpeer(r)).start()
-
-    arrived("ar1", ar1buf.at[pl.ds(1, 7)])
-    d_residual = embedded + sum(ar1buf[r].astype(F32) for r in range(8))
+    part_s[...] = units(nbuf[...]).astype(BF16)
+    for r in t_order:
+        remote("rs2", part_s.at[rows_of(r)], rs2buf.at[r], tpeer(r)).start()
+
+    arrived("datt", dabuf.at[pl.ds(0, 7)])
+    d_all = jnp.concatenate([dabuf[i].astype(F32) for i in range(8)], axis=1)
+    d_residual = embedded + dot(padded(d_all), wo_full[...].reshape(1024, 1024))[0:4]
     ar2buf[0] = units(padded(norm(d_residual, f_gain).astype(F32)))[0:4].astype(BF16)
-    for r in range(1, 8):
+    for r in t_order:
         remote("ar2", ar2buf.at[0], ar2buf.at[r], tpeer(r)).start()
 
-    final = fin_s[...] + part_s[1, my_rows, :].astype(F32)
+    final = res_s[my_rows, :] + part_s[my_rows, :].astype(F32)
     arrived("rs2", rs2buf.at[pl.ds(1, 7)])
     for r in range(1, 8):
         final = final + rs2buf[r].astype(F32)
     out_ref[my_rows, :] = final.astype(BF16)
-    for r in range(1, 8):
+    for r in t_order:
         remote("ag2", out_ref.at[my_rows], out_ref.at[my_rows], tpeer(r)).start()
 
     arrived("ar2", ar2buf.at[pl.ds(1, 7)])
@@ -340,21 +402,25 @@
 
     arrived("relk", relk_ref.at[:, pl.ds(0, 896)])
     arrived("relv", relv_ref.at[:, pl.ds(0, 896)])
-    sent("new", new.at[pl.ds(1, 3)])
+    for d in range(1, 4):
+        sent("new%d" % d, new.at[d])
     sent("past", past.at[pl.ds(1, 3)])
     sent("ids", idall.at[pl.ds(1, 6)])
     sent("q", qbuf.at[pl.ds(1, 3)])
-    sent("e1", e1buf.at[pl.ds(1, 3)])
+    sent("e1", e1buf.at[pl.ds(1, 7)])
     sent("e2", e2buf.at[pl.ds(1, 3)])
-    sent("e3", e3buf.at[pl.ds(1, 7)])
+    sent("e3", e3buf.at[pl.ds(1, 3)])
     sent("relk", relk_ref.at[:, pl.ds(0, 896)])
     sent("relv", relv_ref.at[:, pl.ds(0, 896)])
     sent("part", obuf.at[pl.ds(1, 3)])
     sent("stats", stbuf.at[pl.ds(1, 3)])
     sent("dpart", dbuf.at[pl.ds(1, 3)])
-    sent("rs1", rs1buf.at[pl.ds(1, 7)])
-    sent("ar1", ar1buf.at[pl.ds(1, 7)])
-    sent("ag1", nbuf.at[pl.ds(0, 112)])
+    sent("wo", wo_full.at[pl.ds(0, 3), 0])
+    sent("woz", wo_full.at[0, 0])
+    sent("wof", wo_full.at[pl.ds(0, 3), 0])
+    sent("swap", wo_full.at[:, 0])
+    sent("att", abuf.at[:, pl.ds(0, 896)])
+    sent("datt", dabuf.at[pl.ds(0, 7)])
     sent("rs2", rs2buf.at[pl.ds(1, 7)])
     sent("ar2", ar2buf.at[pl.ds(1, 7)])
     arrived("ag2", out_ref.at[pl.ds(0, 112)])
@@ -379,17 +445,18 @@
     dma = pltpu.SemaphoreType.DMA
     local = [
         ((128, 1024), BF16), ((1024,), BF16), ((1024,), BF16), ((1024,), BF16),
-        ((3, 1024, 128), BF16), ((128, 1024), BF16), ((3, 352, 1024), BF16), ((1024, 251), BF16),
+        ((3, 1024, 128), BF16), ((3, 352, 1024), BF16), ((1024, 251), BF16),
         ((251, 1024), BF16), ((128, 128), BF16),
-        ((128, 128), BF16), ((8, 128, 128), F32), ((1024, 256), F32), ((8, 128), BF16),
-        ((4, 128, 128), BF16), ((4, 8, 128), F32), ((2, 128, 1024), BF16), ((128, 1024), BF16),
-        ((8, 128), BF16), ((16, 1024), F32),
+        ((128, 128), BF16), ((8, 128, 128), F32), ((1024, 256), F32), ((8, 256), F32),
+        ((8, 256), F32), ((128, 256), F32), ((4, 128, 128), BF16), ((4, 8, 128), F32),
+        ((128, 1024), BF16), ((128, 1024), BF16), ((128, 1024), F32),
     ]
     arriving = [
         ((4, 256, 128), BF16), ((4, 256, 128), BF16), ((8, 8, 128), jnp.int32),
         ((4, 128, 128), BF16), ((4, 128, 128), BF16), ((4, 8, 128), F32), ((4, 24, 128), F32),
-        ((4, 4, 1024), BF16), ((4, 4, 1024), BF16), ((8, 4, 1024), BF16),
-        ((8, 16, 1024), BF16), ((8, 4, 1024), BF16), ((8, 16, 1024), BF16), ((8, 4, 1024), BF16),
+        ((8, 4, 1024), BF16), ((4, 4, 1024), BF16), ((4, 4, 1024), BF16),
+        ((8, 2, 64, 1024), BF16), ((128, 1024), BF16), ((8, 4, 128), BF16),
+        ((8, 16, 1024), BF16), ((8, 4, 1024), BF16),
     ]
     shapes = [((128, 1024), BF16), ((4, 251), F32), ((16, 1024), BF16), ((16, 1024), BF16)]
     arrays = [
@@ -406,7 +473,7 @@
         in_specs=[pl.BlockSpec(memory_space=pltpu.SMEM)] + [in_hbm] * 17,
         out_specs=(in_vmem,) * 4,
         scratch_shapes=[pltpu.VMEM(s, d) for s, d in local + arriving]
-        + [dma((17,)), dma((18,)), dma((18,))],
+        + [dma((17,)), dma((23,)), dma((23,))],
         compiler_params=pltpu.CompilerParams(
             collective_id=0, has_side_effects=True, vmem_limit_bytes=60 * 1024 * 1024),
     )(decode_ids, *arrays)

time: 47.8 us -> 41.6 us (0.87)
  Pallas kernels: 47 us -> 40.8 us
    pallas_call x1, Pallas kernels: 46.3 us -> 40 us  [on_device(): pl.pallas_call(kernel, out_shape=tuple((pltpu.VMEM(s, d) for s, d in shap...]
where the time goes in v3:
time: 41.6 us; the launch traced here: 41.4 us
  Pallas kernels  40.8 us (98%)
  between operations  0.65 us (2%)
    pallas_call x1, Pallas kernels, on_device(): pl.pallas_call(kernel, out_shape=tuple((pltpu.VMEM(s, d) for s, d in shap...  40 us

profile of v3, /device:TPU:0, one launch (start us, length us, event | category | flops | bytes accessed | tf_op | source)
XLA Modules:
  0.0 41.4 jit_solution(499385740833138)
XLA Ops:
  0.6 40.0 %shard_map.201 = (bf16[128,1024]{1,0:T(8,128)(2,1)S(1)}, f32[4,251]{1,0:T(4,128)S(1)}, bf16[16,1024]{1,0:T(8,128)(2,1)S(1)}, bf16[16,1024]{1,0:T(8,128)(2,1)S(1)}) custom-call(s32[4]{0:T(128)} %ids_ref.1, bf16[128,1024]{1,0:T(8,128)(2,1)} %x_hbm.1, s32[128]{0:T(128)} %seg_hbm.1, bf16[128,128]{1,0:T(8,128)(2,1)} %pk_hbm.1, bf16[128,128]{1,0:T(8,128)(2,1)} %pv_hbm.1, ...), custom_call_target="tpu_custom_call" | custom-call | tf_op jit(solution)/shard_map/pallas_call | solution.py:470
  40.7 0.8 %shard_map.202 = (bf16[128,1024]{1,0:T(8,128)(2,1)}, f32[4,251]{1,0:T(4,128)}, bf16[16,1024]{1,0:T(8,128)(2,1)}, bf16[16,1024]{1,0:T(8,128)(2,1)}) custom-call(bf16[128,1024]{1,0:T(8,128)(2,1)S(1)} %get-tuple-element.8.refs_0_, f32[4,251]{1,0:T(4,128)S(1)} %get-tuple-element.9.refs_1_, bf16[16,1024]{1,0:T(8,128)(2,1)S(1)} %get-tuple-element.10.refs_2_, ...), custom_call_target="tpu_custom_call" | custom-call | tf_op jit(solution)/shard_map/pallas_call | solution.py:481

commit v4 on v3

--- a/solution.py
+++ b/solution.py
@@ -61,6 +61,10 @@
     def tpeer(r):
         return (c, t_of(r))
 
+    def cpeer(k):
+        return (lax.rem(y + k // 4, 4) * 4 + zc_of(jnp.int32(k % 4)), t)
+
+    c_order = (11, 10, 7, 15, 6, 14, 9, 8, 3, 2, 5, 13, 4, 12, 1)
     y_order = (2, 1, 3)
     z_order = (3, 2, 1)
     t_order = (6, 5, 7, 2, 4, 1, 3)
@@ -128,7 +132,19 @@
     loads["seg"].wait()
     loads["creq"].wait()
 
+    first_row = (c * 8 + t) * 251
+    row16 = lax.broadcasted_iota(jnp.int32, (16, 251), 0)
+    col16 = lax.broadcasted_iota(jnp.int32, (16, 251), 1) + first_row
+    wanted = jnp.full((16, 251), -1, jnp.int32)
+    for q in range(4):
+        wanted = jnp.where(row16 == q, ids_ref[q], wanted)
+    one_hot = (col16 == wanted).astype(F32).astype(BF16)
+    loads["emb"].wait()
+    e1buf[0] = dot(one_hot, emb_v[...])[0:4].astype(BF16)
     pl.semaphore_wait(barrier, 13)
+
+    for r in t_order:
+        remote("e1", e1buf.at[0], e1buf.at[r], tpeer(r)).start()
 
     def send_new(d):
         remote("new%d" % d, new.at[0], new.at[d], ypeer(d)).start()
@@ -144,18 +160,6 @@
     for g in z_order:
         remote("ids", idall.at[0], idall.at[3 + g], zpeer(g)).start()
 
-    first_row = (c * 8 + t) * 251
-    row16 = lax.broadcasted_iota(jnp.int32, (16, 251), 0)
-    col16 = lax.broadcasted_iota(jnp.int32, (16, 251), 1) + first_row
-    wanted = jnp.full((16, 251), -1, jnp.int32)
-    for q in range(4):
-        wanted = jnp.where(row16 == q, ids_ref[q], wanted)
-    one_hot = (col16 == wanted).astype(F32).astype(BF16)
-    loads["emb"].wait()
-    e1buf[0] = dot(one_hot, emb_v[...])[0:4].astype(BF16)
-    for r in t_order:
-        remote("e1", e1buf.at[0], e1buf.at[r], tpeer(r)).start()
-
     remote("woz", wo_hbm.at[my_half], wo_full.at[t, core], tpeer(4)).start()
     for r in (2, 1, 3):
         remote("wo", wo_hbm.at[my_half], wo_full.at[t, core], tpeer(r)).start()
@@ -179,11 +183,6 @@
     across = t_of(4)
     for r in (2, 1, 3):
         remote("wof", wo_full.at[across, core], wo_full.at[across, core], tpeer(r)).start()
-
-    arrived("e1", e1buf.at[pl.ds(1, 7)])
-    e2buf[0] = sum(e1buf[r].astype(F32) for r in range(8)).astype(BF16)
-    for g in z_order:
-        remote("e2", e2buf.at[0], e2buf.at[g], zpeer(g)).start()
 
     arrived("ids", idall.at[pl.ds(1, 6)])
     new_ids = [idall[d, 0:1, :].astype(F32) for d in range(4)]
@@ -194,6 +193,11 @@
         kid_s[b] = jnp.broadcast_to(id_columns[:, b : b + 1], (128, 128))
     idall[7] = idall[0]
     arrived("q", qbuf.at[pl.ds(1, 3)])
+    arrived("e1", e1buf.at[pl.ds(1, 7)])
+    e2buf[0] = sum(e1buf[r].astype(F32) for r in range(8)).astype(BF16)
+    for k in c_order:
+        remote("e2", e2buf.at[0], e2buf.at[k], cpeer(k)).start()
+
     pl.when(y >= 1)(lambda: arrived("new1", new.at[1]))
     pl.when(y >= 2)(lambda: arrived("new2", new.at[2]))
     arrived("past", past.at[pl.ds(1, 3)])
@@ -275,11 +279,6 @@
     lax.fori_loop(0, 4, attend, 0)
     obuf[0] = osend[0]
     stbuf[0] = stsend[0]
-
-    arrived("e2", e2buf.at[pl.ds(1, 3)])
-    e3buf[0] = sum(e2buf[g].astype(F32) for g in range(4)).astype(BF16)
-    for d in y_order:
-        remote("e3", e3buf.at[0], e3buf.at[d], ypeer(d)).start()
 
     arrived("part", obuf.at[pl.ds(1, 3)])
     arrived("stats", stbuf.at[pl.ds(1, 3)])
@@ -300,13 +299,8 @@
     for r in t_order:
         remote("att", abuf.at[:, my_columns], abuf.at[:, my_columns], tpeer(r)).start()
 
-    arrived("wo", wo_full.at[pl.ds(0, 3), 0])
-    arrived("wof", wo_full.at[pl.ds(0, 3), 0])
-    loads["wo"].wait()
-    remote("swap", wo_full.at[:, core], wo_full.at[:, core], zpeer(1)).start()
-
-    arrived("e3", e3buf.at[pl.ds(1, 3)])
-    embedded = sum(e3buf[d].astype(F32) for d in range(4))
+    arrived("e2", e2buf.at[pl.ds(1, 15)])
+    embedded = sum(e2buf[k].astype(F32) for k in range(16))
     pl.when(y < 1)(lambda: arrived("new1", new.at[1]))
     pl.when(y < 2)(lambda: arrived("new2", new.at[2]))
     arrived("new3", new.at[3])
@@ -338,6 +332,22 @@
     for g in z_order:
         remote("dpart", dbuf.at[0], dbuf.at[g], zpeer(g)).start()
 
+    arrived("wo", wo_full.at[pl.ds(0, 3), 0])
+    arrived("wof", wo_full.at[pl.ds(0, 3), 0])
+    loads["wo"].wait()
+    remote("swap", wo_full.at[:, core], wo_full.at[:, core], zpeer(1)).start()
+
+    def units(rows):
+        gate = dot_nt(rows, ffn_v[0])
+        up = dot_nt(rows, ffn_v[1])
+        hidden = (jax.nn.gelu(gate, approximate=True) * up).astype(BF16)
+        return dot(hidden, ffn_v[2])
+
+    arrived("swap", wo_full.at[:, 0])
+    arrived("att", abuf.at[:, pl.ds(0, 896)])
+    residual = x_v[...].astype(F32) + dot(abuf[...], wo_full[...].reshape(1024, 1024))
+    res_s[...] = residual
+
     own_m = jnp.sum(qd8 * jnp.concatenate([dk, dk], axis=0), axis=1, keepdims=True)
     own_m = jnp.broadcast_to(own_m, (8, 128))
     arrived("dpart", dbuf.at[pl.ds(1, 3)])
@@ -358,16 +368,6 @@
     for r in t_order:
         remote("datt", dabuf.at[t], dabuf.at[t], tpeer(r)).start()
 
-    def units(rows):
-        gate = dot_nt(rows, ffn_v[0])
-        up = dot_nt(rows, ffn_v[1])
-        hidden = (jax.nn.gelu(gate, approximate=True) * up).astype(BF16)
-        return dot(hidden, ffn_v[2])
-
-    arrived("swap", wo_full.at[:, 0])
-    arrived("att", abuf.at[:, pl.ds(0, 896)])
-    residual = x_v[...].astype(F32) + dot(abuf[...], wo_full[...].reshape(1024, 1024))
-    res_s[...] = residual
     loads["fg"].wait()
     f_gain = gain_of(fg_v)
     nbuf[...] = norm(residual, f_gain)
@@ -408,8 +408,7 @@
     sent("ids", idall.at[pl.ds(1, 6)])
     sent("q", qbuf.at[pl.ds(1, 3)])
     sent("e1", e1buf.at[pl.ds(1, 7)])
-    sent("e2", e2buf.at[pl.ds(1, 3)])
-    sent("e3", e3buf.at[pl.ds(1, 3)])
+    sent("e2", e2buf.at[pl.ds(1, 15)])
     sent("relk", relk_ref.at[:, pl.ds(0, 896)])
     sent("relv", relv_ref.at[:, pl.ds(0, 896)])
     sent("part", obuf.at[pl.ds(1, 3)])
@@ -454,7 +453,7 @@
     arriving = [
         ((4, 256, 128), BF16), ((4, 256, 128), BF16), ((8, 8, 128), jnp.int32),
         ((4, 128, 128), BF16), ((4, 128, 128), BF16), ((4, 8, 128), F32), ((4, 24, 128), F32),
-        ((8, 4, 1024), BF16), ((4, 4, 1024), BF16), ((4, 4, 1024), BF16),
+        ((8, 4, 1024), BF16), ((16, 4, 1024), BF16), ((4, 4, 1024), BF16),
         ((8, 2, 64, 1024), BF16), ((128, 1024), BF16), ((8, 4, 128), BF16),
         ((8, 16, 1024), BF16), ((8, 4, 1024), BF16),
     ]

time: 41.6 us -> 38.8 us (0.933)
  Pallas kernels: 40.8 us -> 38 us
    pallas_call x1, Pallas kernels: 40 us -> 37.2 us  [on_device(): pl.pallas_call(kernel, out_shape=tuple((pltpu.VMEM(s, d) for s, d in shap...]
where the time goes in v4:
time: 38.8 us; the launch traced here: 38.7 us
  Pallas kernels  38 us (98%)
  between operations  0.65 us (2%)
    pallas_call x1, Pallas kernels, on_device(): pl.pallas_call(kernel, out_shape=tuple((pltpu.VMEM(s, d) for s, d in shap...  37.2 us

profile of v4, /device:TPU:0, one launch (start us, length us, event | category | flops | bytes accessed | tf_op | source)
XLA Modules:
  0.0 38.7 jit_solution(17170418404311462620)
XLA Ops:
  0.6 37.2 %shard_map.201 = (bf16[128,1024]{1,0:T(8,128)(2,1)S(1)}, f32[4,251]{1,0:T(4,128)S(1)}, bf16[16,1024]{1,0:T(8,128)(2,1)S(1)}, bf16[16,1024]{1,0:T(8,128)(2,1)S(1)}) custom-call(s32[4]{0:T(128)} %ids_ref.1, bf16[128,1024]{1,0:T(8,128)(2,1)} %x_hbm.1, s32[128]{0:T(128)} %seg_hbm.1, bf16[128,128]{1,0:T(8,128)(2,1)} %pk_hbm.1, bf16[128,128]{1,0:T(8,128)(2,1)} %pv_hbm.1, ...), custom_call_target="tpu_custom_call" | custom-call | tf_op jit(solution)/shard_map/pallas_call | solution.py:469
  37.9 0.8 %shard_map.202 = (bf16[128,1024]{1,0:T(8,128)(2,1)}, f32[4,251]{1,0:T(4,128)}, bf16[16,1024]{1,0:T(8,128)(2,1)}, bf16[16,1024]{1,0:T(8,128)(2,1)}) custom-call(bf16[128,1024]{1,0:T(8,128)(2,1)S(1)} %get-tuple-element.8.refs_0_, f32[4,251]{1,0:T(4,128)S(1)} %get-tuple-element.9.refs_1_, bf16[16,1024]{1,0:T(8,128)(2,1)S(1)} %get-tuple-element.10.refs_2_, ...), custom_call_target="tpu_custom_call" | custom-call | tf_op jit(solution)/shard_map/pallas_call | solution.py:480

commit v5 on v4

--- a/solution.py
+++ b/solution.py
@@ -71,7 +71,7 @@
 
     names = (
         "past", "new1", "new2", "new3", "ids", "q", "e1", "e2", "e3", "relk", "relv",
-        "part", "stats", "dpart", "wo", "woz", "wof", "swap", "att", "datt", "rs2", "ar2", "ag2",
+        "part", "stats", "dpart", "wo", "woz", "wof", "swap", "att", "datt", "rs2a", "rs2b", "ar2", "ag2",
     )
 
     def remote(name, src, dst, peer):
@@ -337,11 +337,14 @@
     loads["wo"].wait()
     remote("swap", wo_full.at[:, core], wo_full.at[:, core], zpeer(1)).start()
 
-    def units(rows):
+    half = (pl.ds(0, 512), pl.ds(512, 512))
+    def hidden_of(rows):
         gate = dot_nt(rows, ffn_v[0])
         up = dot_nt(rows, ffn_v[1])
-        hidden = (jax.nn.gelu(gate, approximate=True) * up).astype(BF16)
-        return dot(hidden, ffn_v[2])
+        return (jax.nn.gelu(gate, approximate=True) * up).astype(BF16)
+
+    def units(rows):
+        return dot(hidden_of(rows), ffn_v[2])
 
     arrived("swap", wo_full.at[:, 0])
     arrived("att", abuf.at[:, pl.ds(0, 896)])
@@ -374,9 +377,12 @@
     loads["wg"].wait()
     loads["wu"].wait()
     loads["wd"].wait()
-    part_s[...] = units(nbuf[...]).astype(BF16)
-    for r in t_order:
-        remote("rs2", part_s.at[rows_of(r)], rs2buf.at[r], tpeer(r)).start()
+    hidden = hidden_of(nbuf[...])
+    for h in range(2):
+        part_s[:, half[h]] = dot(hidden, ffn_v[2, :, half[h]]).astype(BF16)
+        for r in t_order:
+            remote("rs2" + "ab"[h], part_s.at[rows_of(r), half[h]], rs2buf.at[r, :, half[h]],
+                   tpeer(r)).start()
 
     arrived("datt", dabuf.at[pl.ds(0, 7)])
     d_all = jnp.concatenate([dabuf[i].astype(F32) for i in range(8)], axis=1)
@@ -385,13 +391,15 @@
     for r in t_order:
         remote("ar2", ar2buf.at[0], ar2buf.at[r], tpeer(r)).start()
 
-    final = res_s[my_rows, :] + part_s[my_rows, :].astype(F32)
-    arrived("rs2", rs2buf.at[pl.ds(1, 7)])
-    for r in range(1, 8):
-        final = final + rs2buf[r].astype(F32)
-    out_ref[my_rows, :] = final.astype(BF16)
-    for r in t_order:
-        remote("ag2", out_ref.at[my_rows], out_ref.at[my_rows], tpeer(r)).start()
+    for h in range(2):
+        final = res_s[my_rows, half[h]] + part_s[my_rows, half[h]].astype(F32)
+        arrived("rs2" + "ab"[h], rs2buf.at[pl.ds(1, 7), :, half[h]])
+        for r in range(1, 8):
+            final = final + rs2buf[r, :, half[h]].astype(F32)
+        out_ref[my_rows, half[h]] = final.astype(BF16)
+        for r in t_order:
+            remote("ag2", out_ref.at[my_rows, half[h]], out_ref.at[my_rows, half[h]],
+                   tpeer(r)).start()
 
     arrived("ar2", ar2buf.at[pl.ds(1, 7)])
     d_final = d_residual + sum(ar2buf[r].astype(F32) for r in range(8))
@@ -420,7 +428,8 @@
     sent("swap", wo_full.at[:, 0])
     sent("att", abuf.at[:, pl.ds(0, 896)])
     sent("datt", dabuf.at[pl.ds(0, 7)])
-    sent("rs2", rs2buf.at[pl.ds(1, 7)])
+    sent("rs2a", rs2buf.at[pl.ds(1, 7), :, half[0]])
+    sent("rs2b", rs2buf.at[pl.ds(1, 7), :, half[1]])
     sent("ar2", ar2buf.at[pl.ds(1, 7)])
     arrived("ag2", out_ref.at[pl.ds(0, 112)])
     sent("ag2", out_ref.at[pl.ds(0, 112)])
@@ -472,7 +481,7 @@
         in_specs=[pl.BlockSpec(memory_space=pltpu.SMEM)] + [in_hbm] * 17,
         out_specs=(in_vmem,) * 4,
         scratch_shapes=[pltpu.VMEM(s, d) for s, d in local + arriving]
-        + [dma((17,)), dma((23,)), dma((23,))],
+        + [dma((17,)), dma((24,)), dma((24,))],
         compiler_params=pltpu.CompilerParams(
             collective_id=0, has_side_effects=True, vmem_limit_bytes=60 * 1024 * 1024),
     )(decode_ids, *arrays)

time: 38.8 us -> 38.5 us (level)
  no operation moved by 1% of the time
where the time goes in v5:
time: 38.5 us; the launch traced here: 38.4 us
  Pallas kernels  37.7 us (98%)
  between operations  0.65 us (2%)
    pallas_call x1, Pallas kernels, on_device(): pl.pallas_call(kernel, out_shape=tuple((pltpu.VMEM(s, d) for s, d in shap...  37 us

profile of v5, /device:TPU:0, one launch (start us, length us, event | category | flops | bytes accessed | tf_op | source)
XLA Modules:
  0.0 38.4 jit_solution(6829330741696842050)
XLA Ops:
  0.6 37.0 %shard_map.201 = (bf16[128,1024]{1,0:T(8,128)(2,1)S(1)}, f32[4,251]{1,0:T(4,128)S(1)}, bf16[16,1024]{1,0:T(8,128)(2,1)S(1)}, bf16[16,1024]{1,0:T(8,128)(2,1)S(1)}) custom-call(s32[4]{0:T(128)} %ids_ref.1, bf16[128,1024]{1,0:T(8,128)(2,1)} %x_hbm.1, s32[128]{0:T(128)} %seg_hbm.1, bf16[128,128]{1,0:T(8,128)(2,1)} %pk_hbm.1, bf16[128,128]{1,0:T(8,128)(2,1)} %pv_hbm.1, ...), custom_call_target="tpu_custom_call" | custom-call | tf_op jit(solution)/shard_map/pallas_call | solution.py:478
  37.6 0.8 %shard_map.202 = (bf16[128,1024]{1,0:T(8,128)(2,1)}, f32[4,251]{1,0:T(4,128)}, bf16[16,1024]{1,0:T(8,128)(2,1)}, bf16[16,1024]{1,0:T(8,128)(2,1)}) custom-call(bf16[128,1024]{1,0:T(8,128)(2,1)S(1)} %get-tuple-element.8.refs_0_, f32[4,251]{1,0:T(4,128)S(1)} %get-tuple-element.9.refs_1_, bf16[16,1024]{1,0:T(8,128)(2,1)S(1)} %get-tuple-element.10.refs_2_, ...), custom_call_target="tpu_custom_call" | custom-call | tf_op jit(solution)/shard_map/pallas_call | solution.py:489

commit v6 on v5

--- a/solution.py
+++ b/solution.py
@@ -71,7 +71,7 @@
 
     names = (
         "past", "new1", "new2", "new3", "ids", "q", "e1", "e2", "e3", "relk", "relv",
-        "part", "stats", "dpart", "wo", "woz", "wof", "swap", "att", "datt", "rs2a", "rs2b", "ar2", "ag2",
+        "part", "stats", "dpart", "wo", "woz", "wof", "swap", "att", "datt", "rs2a", "rs2b", "rs2c", "rs2d", "ar2", "ag2",
     )
 
     def remote(name, src, dst, peer):
@@ -337,7 +337,7 @@
     loads["wo"].wait()
     remote("swap", wo_full.at[:, core], wo_full.at[:, core], zpeer(1)).start()
 
-    half = (pl.ds(0, 512), pl.ds(512, 512))
+    half = (pl.ds(0, 256), pl.ds(256, 256), pl.ds(512, 256), pl.ds(768, 256))
     def hidden_of(rows):
         gate = dot_nt(rows, ffn_v[0])
         up = dot_nt(rows, ffn_v[1])
@@ -378,10 +378,10 @@
     loads["wu"].wait()
     loads["wd"].wait()
     hidden = hidden_of(nbuf[...])
-    for h in range(2):
+    for h in range(4):
         part_s[:, half[h]] = dot(hidden, ffn_v[2, :, half[h]]).astype(BF16)
         for r in t_order:
-            remote("rs2" + "ab"[h], part_s.at[rows_of(r), half[h]], rs2buf.at[r, :, half[h]],
+            remote("rs2" + "abcd"[h], part_s.at[rows_of(r), half[h]], rs2buf.at[r, :, half[h]],
                    tpeer(r)).start()
 
     arrived("datt", dabuf.at[pl.ds(0, 7)])
@@ -391,9 +391,9 @@
     for r in t_order:
         remote("ar2", ar2buf.at[0], ar2buf.at[r], tpeer(r)).start()
 
-    for h in range(2):
+    for h in range(4):
         final = res_s[my_rows, half[h]] + part_s[my_rows, half[h]].astype(F32)
-        arrived("rs2" + "ab"[h], rs2buf.at[pl.ds(1, 7), :, half[h]])
+        arrived("rs2" + "abcd"[h], rs2buf.at[pl.ds(1, 7), :, half[h]])
         for r in range(1, 8):
             final = final + rs2buf[r, :, half[h]].astype(F32)
         out_ref[my_rows, half[h]] = final.astype(BF16)
@@ -430,6 +430,8 @@
     sent("datt", dabuf.at[pl.ds(0, 7)])
     sent("rs2a", rs2buf.at[pl.ds(1, 7), :, half[0]])
     sent("rs2b", rs2buf.at[pl.ds(1, 7), :, half[1]])
+    sent("rs2c", rs2buf.at[pl.ds(1, 7), :, half[2]])
+    sent("rs2d", rs2buf.at[pl.ds(1, 7), :, half[3]])
     sent("ar2", ar2buf.at[pl.ds(1, 7)])
     arrived("ag2", out_ref.at[pl.ds(0, 112)])
     sent("ag2", out_ref.at[pl.ds(0, 112)])
@@ -481,7 +483,7 @@
         in_specs=[pl.BlockSpec(memory_space=pltpu.SMEM)] + [in_hbm] * 17,
         out_specs=(in_vmem,) * 4,
         scratch_shapes=[pltpu.VMEM(s, d) for s, d in local + arriving]
-        + [dma((17,)), dma((24,)), dma((24,))],
+        + [dma((17,)), dma((26,)), dma((26,))],
         compiler_params=pltpu.CompilerParams(
             collective_id=0, has_side_effects=True, vmem_limit_bytes=60 * 1024 * 1024),
     )(decode_ids, *arrays)

time: 38.5 us -> 38.5 us (level)
  no operation moved by 1% of the time
where the time goes in v6:
time: 38.5 us; the launch traced here: 38.4 us
  Pallas kernels  37.7 us (98%)
  between operations  0.65 us (2%)
    pallas_call x1, Pallas kernels, on_device(): pl.pallas_call(kernel, out_shape=tuple((pltpu.VMEM(s, d) for s, d in shap...  37 us

profile of v6, /device:TPU:0, one launch (start us, length us, event | category | flops | bytes accessed | tf_op | source)
XLA Modules:
  0.0 38.4 jit_solution(1783504848411902970)
XLA Ops:
  0.6 37.0 %shard_map.201 = (bf16[128,1024]{1,0:T(8,128)(2,1)S(1)}, f32[4,251]{1,0:T(4,128)S(1)}, bf16[16,1024]{1,0:T(8,128)(2,1)S(1)}, bf16[16,1024]{1,0:T(8,128)(2,1)S(1)}) custom-call(s32[4]{0:T(128)} %ids_ref.1, bf16[128,1024]{1,0:T(8,128)(2,1)} %x_hbm.1, s32[128]{0:T(128)} %seg_hbm.1, bf16[128,128]{1,0:T(8,128)(2,1)} %pk_hbm.1, bf16[128,128]{1,0:T(8,128)(2,1)} %pv_hbm.1, ...), custom_call_target="tpu_custom_call" | custom-call | tf_op jit(solution)/shard_map/pallas_call | solution.py:480
  37.6 0.8 %shard_map.202 = (bf16[128,1024]{1,0:T(8,128)(2,1)}, f32[4,251]{1,0:T(4,128)}, bf16[16,1024]{1,0:T(8,128)(2,1)}, bf16[16,1024]{1,0:T(8,128)(2,1)}) custom-call(bf16[128,1024]{1,0:T(8,128)(2,1)S(1)} %get-tuple-element.8.refs_0_, f32[4,251]{1,0:T(4,128)S(1)} %get-tuple-element.9.refs_1_, bf16[16,1024]{1,0:T(8,128)(2,1)S(1)} %get-tuple-element.10.refs_2_, ...), custom_call_target="tpu_custom_call" | custom-call | tf_op jit(solution)/shard_map/pallas_call | solution.py:491

commit v7 on v6

--- a/solution.py
+++ b/solution.py
@@ -71,7 +71,7 @@
 
     names = (
         "past", "new1", "new2", "new3", "ids", "q", "e1", "e2", "e3", "relk", "relv",
-        "part", "stats", "dpart", "wo", "woz", "wof", "swap", "att", "datt", "rs2a", "rs2b", "rs2c", "rs2d", "ar2", "ag2",
+        "part", "stats", "dpart", "wo", "woz", "wof", "swap", "swap2", "att", "datt", "rs2a", "rs2b", "rs2c", "rs2d", "ar2", "ag2",
     )
 
     def remote(name, src, dst, peer):
@@ -279,6 +279,12 @@
     lax.fori_loop(0, 4, attend, 0)
     obuf[0] = osend[0]
     stbuf[0] = stsend[0]
+
+    near = pl.ds(z_lo * 4, 4)
+    far = pl.ds((1 - z_lo) * 4, 4)
+    arrived("wo", wo_full.at[pl.ds(0, 3), 0])
+    loads["wo"].wait()
+    remote("swap", wo_full.at[near, core], wo_full.at[near, core], zpeer(1)).start()
 
     arrived("part", obuf.at[pl.ds(1, 3)])
     arrived("stats", stbuf.at[pl.ds(1, 3)])
@@ -332,10 +338,8 @@
     for g in z_order:
         remote("dpart", dbuf.at[0], dbuf.at[g], zpeer(g)).start()
 
-    arrived("wo", wo_full.at[pl.ds(0, 3), 0])
     arrived("wof", wo_full.at[pl.ds(0, 3), 0])
-    loads["wo"].wait()
-    remote("swap", wo_full.at[:, core], wo_full.at[:, core], zpeer(1)).start()
+    remote("swap2", wo_full.at[far, core], wo_full.at[far, core], zpeer(1)).start()
 
     half = (pl.ds(0, 256), pl.ds(256, 256), pl.ds(512, 256), pl.ds(768, 256))
     def hidden_of(rows):
@@ -346,9 +350,14 @@
     def units(rows):
         return dot(hidden_of(rows), ffn_v[2])
 
-    arrived("swap", wo_full.at[:, 0])
+    arrived("swap", wo_full.at[pl.ds(0, 4), 0])
     arrived("att", abuf.at[:, pl.ds(0, 896)])
-    residual = x_v[...].astype(F32) + dot(abuf[...], wo_full[...].reshape(1024, 1024))
+    near_lanes = pl.ds(pl.multiple_of(z_lo * 512, 512), 512)
+    far_lanes = pl.ds(pl.multiple_of((1 - z_lo) * 512, 512), 512)
+    residual = x_v[...].astype(F32) + dot(
+        abuf[:, near_lanes], wo_full[near].reshape(512, 1024))
+    arrived("swap2", wo_full.at[pl.ds(0, 4), 0])
+    residual = residual + dot(abuf[:, far_lanes], wo_full[far].reshape(512, 1024))
     res_s[...] = residual
 
     own_m = jnp.sum(qd8 * jnp.concatenate([dk, dk], axis=0), axis=1, keepdims=True)
@@ -425,7 +434,8 @@
     sent("wo", wo_full.at[pl.ds(0, 3), 0])
     sent("woz", wo_full.at[0, 0])
     sent("wof", wo_full.at[pl.ds(0, 3), 0])
-    sent("swap", wo_full.at[:, 0])
+    sent("swap", wo_full.at[pl.ds(0, 4), 0])
+    sent("swap2", wo_full.at[pl.ds(0, 4), 0])
     sent("att", abuf.at[:, pl.ds(0, 896)])
     sent("datt", dabuf.at[pl.ds(0, 7)])
     sent("rs2a", rs2buf.at[pl.ds(1, 7), :, half[0]])
@@ -483,7 +493,7 @@
         in_specs=[pl.BlockSpec(memory_space=pltpu.SMEM)] + [in_hbm] * 17,
         out_specs=(in_vmem,) * 4,
         scratch_shapes=[pltpu.VMEM(s, d) for s, d in local + arriving]
-        + [dma((17,)), dma((26,)), dma((26,))],
+        + [dma((17,)), dma((27,)), dma((27,))],
         compiler_params=pltpu.CompilerParams(
             collective_id=0, has_side_effects=True, vmem_limit_bytes=60 * 1024 * 1024),
     )(decode_ids, *arrays)

time: 38.5 us -> 38.7 us (level)
  no operation moved by 1% of the time
where the time goes in v7:
time: 38.7 us; the launch traced here: 38.6 us
  Pallas kernels  38 us (98%)
  between operations  0.65 us (2%)
    pallas_call x1, Pallas kernels, on_device(): pl.pallas_call(kernel, out_shape=tuple((pltpu.VMEM(s, d) for s, d in shap...  37.2 us

profile of v7, /device:TPU:0, one launch (start us, length us, event | category | flops | bytes accessed | tf_op | source)
XLA Modules:
  0.0 38.6 jit_solution(4979147859356002012)
XLA Ops:
  0.6 37.2 %shard_map.201 = (bf16[128,1024]{1,0:T(8,128)(2,1)S(1)}, f32[4,251]{1,0:T(4,128)S(1)}, bf16[16,1024]{1,0:T(8,128)(2,1)S(1)}, bf16[16,1024]{1,0:T(8,128)(2,1)S(1)}) custom-call(s32[4]{0:T(128)} %ids_ref.1, bf16[128,1024]{1,0:T(8,128)(2,1)} %x_hbm.1, s32[128]{0:T(128)} %seg_hbm.1, bf16[128,128]{1,0:T(8,128)(2,1)} %pk_hbm.1, bf16[128,128]{1,0:T(8,128)(2,1)} %pv_hbm.1, ...), custom_call_target="tpu_custom_call" | custom-call | tf_op jit(solution)/shard_map/pallas_call | solution.py:490
  37.8 0.8 %shard_map.202 = (bf16[128,1024]{1,0:T(8,128)(2,1)}, f32[4,251]{1,0:T(4,128)}, bf16[16,1024]{1,0:T(8,128)(2,1)}, bf16[16,1024]{1,0:T(8,128)(2,1)}) custom-call(bf16[128,1024]{1,0:T(8,128)(2,1)S(1)} %get-tuple-element.8.refs_0_, f32[4,251]{1,0:T(4,128)S(1)} %get-tuple-element.9.refs_1_, bf16[16,1024]{1,0:T(8,128)(2,1)S(1)} %get-tuple-element.10.refs_2_, ...), custom_call_target="tpu_custom_call" | custom-call | tf_op jit(solution)/shard_map/pallas_call | solution.py:501
